TPU v7x, 32 devices: a whole 2x2x4 slice. The times are simulated.
32 devices in a mesh: ctx: 8 (over z, y), head: 4 (over x, core).
Axes of the slice: x: 2, y: 2, z: 4, core: 2. Of those that a mesh axis runs over, the one named last changes fastest.
Arguments:
- qkv: bfloat16 [3, 4096, 5120], P(None, 'ctx', 'head'), may hold values from -8 to 8
- step_size: float32 [4096, 8], P('ctx', 'head'), may hold values from 0.01 to 0.1
- fast_in: bfloat16 [8, 640, 1024], P('head'), may hold values from -1 to 1
- fast_out: bfloat16 [8, 512, 640], P('head'), may hold values from -1 to 1
Outputs:
- mixed: bfloat16 [4096, 5120], P('ctx', 'head')
All inputs are finite; a program needn't handle non-finite values.
Results may differ from a plain program's by a relative error of at most 0.0087.
Values may be sent and summed in bfloat16 or wider, within the bound.
No kernel may reach another device: no remote copies, remote signals or barrier semaphores. Data moves between devices by JAX's collectives and lax.ppermute only.
A program may use at most 128 MiB of HBM per device.

v0:
```python
import jax
import jax.numpy as jnp
from jax import lax
from jax.sharding import PartitionSpec as P

ADIM = 128


EPS = 1e-06


def shifted(array, axis, by):
    size = lax.axis_size(axis)
    pairs = [(i, i + by) for i in range(size) if 0 <= i + by < size]
    return lax.ppermute(array, axis, pairs)


def silu_parts(gate_part):
    sigmoid_part = jax.nn.sigmoid(gate_part)
    return (gate_part * sigmoid_part, sigmoid_part * (1.0 + gate_part * (1.0 - sigmoid_part)))


def renorm(weight, update, norm_axis):
    old_value = weight.astype(jnp.float32)
    moved_value = old_value + update
    old_norm = jnp.sqrt(jnp.sum(old_value * old_value, axis=norm_axis, keepdims=True))
    new_norm = jnp.sqrt(jnp.sum(moved_value * moved_value, axis=norm_axis, keepdims=True))
    return (moved_value * (old_norm / (new_norm + EPS))).astype(jnp.bfloat16)


def local(qkv, step_size, fast_in, fast_out):
    tok_rows = qkv.shape[1]
    col_width = qkv.shape[2]
    per_device = fast_in.shape[0]
    head_width = fast_in.shape[1]
    hidden_dim = fast_out.shape[1]
    ctx_count = lax.axis_size("ctx")
    queries = qkv[0]
    key_rows = qkv[1]
    values = qkv[2]
    own_pair = qkv[1:]
    near_pair = shifted(own_pair, "ctx", 1)
    far_pair = shifted(own_pair, "ctx", 2)
    window_pair = jnp.concatenate([far_pair, near_pair, own_pair], axis=1)
    seq_start = lax.axis_index("ctx") * tok_rows
    row_pos = lax.broadcasted_iota(jnp.int32, (tok_rows, 3 * tok_rows), 0)
    col_pos = lax.broadcasted_iota(jnp.int32, (tok_rows, 3 * tok_rows), 1)
    allowed = (
        (col_pos > row_pos)
        & (col_pos <= row_pos + 2 * tok_rows)
        & (col_pos + seq_start >= 2 * tok_rows)
    )

    def one_head(head_index):
        offset = head_index * ADIM
        query_head = lax.dynamic_slice_in_dim(queries, offset, ADIM, 1)
        window_head = lax.dynamic_slice_in_dim(window_pair, offset, ADIM, 2)
        scores = jnp.dot(
            query_head, window_head[0].T, preferred_element_type=jnp.float32
        ) * ADIM ** (-0.5)
        scores = jnp.where(allowed, scores, -1e30)
        row_max = jnp.max(scores, axis=-1, keepdims=True)
        weights = jnp.where(allowed, jnp.exp(scores - row_max), 0.0)
        row_total = jnp.sum(weights, axis=-1, keepdims=True)
        probs_bf = (weights / row_total).astype(jnp.bfloat16)
        return jnp.dot(probs_bf, window_head[1], preferred_element_type=jnp.float32)

    head_count = col_width // ADIM
    attended = lax.map(one_head, jnp.arange(head_count, dtype=jnp.int32))
    attended = attended.transpose(1, 0, 2).reshape(tok_rows, col_width)
    query_three = queries.reshape(tok_rows, per_device, head_width)
    key_three = key_rows.reshape(tok_rows, per_device, head_width)
    value_three = values.reshape(tok_rows, per_device, head_width)
    projected = jnp.einsum("thd,hdf->thf", key_three, fast_in, preferred_element_type=jnp.float32)
    gate_part = projected[..., :hidden_dim]
    up_part = projected[..., hidden_dim:]
    activated, slope_part = silu_parts(gate_part)
    hidden = (activated * up_part).astype(jnp.bfloat16)
    scaled = (step_size[:, :, None] * value_three.astype(jnp.float32)).astype(jnp.bfloat16)
    back_part = jnp.einsum("thd,hfd->thf", scaled, fast_out, preferred_element_type=jnp.float32)
    pre_grad = jnp.concatenate(
        [back_part * up_part * slope_part, back_part * activated], axis=2
    ).astype(jnp.bfloat16)
    factor = (tok_rows * ctx_count) ** (-0.5)
    grad_in = jnp.einsum("thd,thf->hdf", key_three, pre_grad, preferred_element_type=jnp.float32)
    grad_out = jnp.einsum("thf,thd->hfd", hidden, scaled, preferred_element_type=jnp.float32)
    grad_in, grad_out = lax.psum((grad_in, grad_out), "ctx")
    new_in = renorm(fast_in, grad_in * factor, 1)
    new_out = renorm(fast_out, grad_out * factor, 1)
    query_proj = jnp.einsum("thd,hdf->thf", query_three, new_in, preferred_element_type=jnp.float32)
    query_act, unused_slope = silu_parts(query_proj[..., :hidden_dim])
    query_hidden = (query_act * query_proj[..., hidden_dim:]).astype(jnp.bfloat16)
    applied = jnp.einsum("thf,hfd->thd", query_hidden, new_out, preferred_element_type=jnp.float32)
    applied = applied.reshape(tok_rows, col_width)
    return (attended + applied).astype(jnp.bfloat16)


def solution(mesh):
    placed = (
        P(None, "ctx", "head"),
        P("ctx", "head"),
        P("head", None, None),
        P("head", None, None),
    )
    return jax.shard_map(
        local, mesh=mesh, in_specs=placed, out_specs=P("ctx", "head"), check_vma=False
    )
```

profile of v0, /device:TPU:0, one launch (start us, length us, event | category | flops | bytes accessed | tf_op | source)
XLA Modules:
  0.0 394.0 jit_solution(16632205564670657775)
XLA Ops:
  6.5 3.5 slice.31
  10.1 6.4 %collective-permute-start = (bf16[2,512,1280]{2,1,0:T(8,128)(2,1)}, bf16[2,512,1280]{2,1,0:T(8,128)(2,1)}, u32[]{:S(2)}, u32[]{:S(2)}) collective-permute-start(bf16[2,512,1280]{2,1,0:T(8,128)(2,1)} %slice.31), channel_id=1, source_target_pairs={{0,8},{4,12},{8,16},{12,20},{16,24},{20,28},{1,9},{5,13},{9,17},{1... | collective-permute-start | bytes 7864328 | tf_op jit(solution)/shard_map/ppermute | solution.py:15
  16.5 5.0 %collective-permute-start.1 = (bf16[2,512,1280]{2,1,0:T(8,128)(2,1)}, bf16[2,512,1280]{2,1,0:T(8,128)(2,1)}, u32[]{:S(2)}, u32[]{:S(2)}) collective-permute-start(bf16[2,512,1280]{2,1,0:T(8,128)(2,1)} %slice.31), channel_id=1, source_target_pairs={{0,4},{4,8},{8,12},{12,16},{16,20},{20,24},{24,28},{1,5},{5,9},{9,... | collective-permute-start | bytes 7864328 | tf_op jit(solution)/shard_map/ppermute | solution.py:15
  24.4 4.3 %reshape.39 = f32[512,2,640]{2,1,0:T(2,128)} reshape(f32[1,512,1280]{2,1,0:T(8,128)} %get-tuple-element.89) | data formatting | bytes 5242880 | tf_op jit(solution)/shard_map/convert_element_type | solution.py:79
  28.7 3.7 convolution_bitcast_fusion.1
  34.5 4.1 %convolution_bitcast_fusion = f32[2,640,1024]{1,2,0:T(8,128)} fusion(bf16[512,2,640]{0,2,1:T(8,128)(2,1)S(1)} %bitcast.57, bf16[512,2,512]{0,2,1:T(8,128)(2,1)S(1)} %get-tuple-element.86, bf16[512,2,512]{0,2,1:T(8,128)(2,1)S(1)} %get-tuple-element.85), kind=kOutput, calls=%fused_computation.37 | convolution fusion | flops 1346371584 | bytes 8650752 | tf_op jit(solution)/shard_map/thd,thf->hdf/dot_general | solution.py:85
  38.6 2.6 fusion.32
  42.9 2.6 copy.19
  45.6 2.5 copy.34
  48.1 52.0 %collective-permute-done = bf16[2,512,1280]{2,1,0:T(8,128)(2,1)} collective-permute-done((bf16[2,512,1280]{2,1,0:T(8,128)(2,1)}, bf16[2,512,1280]{2,1,0:T(8,128)(2,1)}, u32[]{:S(2)}, u32[]{:S(2)}) %collective-permute-start) | collective-permute-done | bytes 2621472 | tf_op jit(solution)/shard_map/ppermute | solution.py:15
  100.0 7.0 %pad_maximum_fusion = bf16[2,1536,1280]{2,1,0:T(8,128)(2,1)} fusion(bf16[2,512,1280]{2,1,0:T(8,128)(2,1)} %slice.31, bf16[2,512,1280]{2,1,0:T(8,128)(2,1)} %collective-permute-done.1, bf16[2,512,1280]{2,1,0:T(8,128)(2,1)} %collective-permute-done), kind=kLoop, calls=%fused_computation.19 | loop fusion | flops 23592960 | bytes 15728640 | tf_op jit(solution)/shard_map/concatenate | solution.py:44
  107.0 84.5 %while.11 = (s32[]{:T(128)}, f32[10,512,128]{1,2,0:T(8,128)}, s32[10]{0:T(128)S(1)}, bf16[512,1280]{0,1:T(8,128)(2,1)}, bf16[2,1536,1280]{2,1,0:T(8,128)(2,1)}, ...) while((s32[]{:T(128)}, f32[10,512,128]{1,2,0:T(8,128)}, ...), condition=%wide.region_3.4_spmd.clone, body=%wide.region_0.3_spmd.clone.sunk | while | flops 419953664 | bytes 10639555 | solution.py:69
  108.2 2.3 fusion.53
  111.7 3.7 fusion.55
  116.7 2.3 fusion.53
  120.1 3.7 fusion.55
  125.1 2.3 fusion.53
  128.5 3.7 fusion.55
  133.5 2.3 fusion.53
  137.0 3.7 fusion.55
  142.0 2.3 fusion.53
  145.5 3.7 fusion.55
  153.9 3.7 fusion.55
  158.9 2.3 fusion.53
  162.3 3.7 fusion.55
  170.8 3.7 fusion.55
  179.2 3.7 fusion.55
  184.2 2.3 fusion.53
  187.7 3.8 fusion.55
  191.4 182.6 %all-reduce.3.cloned.1.call-done = (f32[2,512,640]{2,1,0:T(8,128)}, f32[2,640,1024]{1,2,0:T(8,128)}) async-done(((f32[2,512,640]{2,1,0:T(8,128)}, f32[2,640,1024]{1,2,0:T(8,128)}), (f32[2,512,640]{2,1,0:T(8,128)}, f32[2,640,1024]{1,2,0:T(8,128)})) %all-reduce.3.cloned.1.call-update) | async-done | bytes 7864336 | tf_op jit(solution)/shard_map/psum | solution.py:87
  374.1 2.8 fusion.14
  376.9 3.9 fusion.13
  (61 shorter events, 37.5 us)
Async XLA Ops:
  6.5 367.5 %all-reduce.3.cloned.1.call-start = ((), (), s32[]{:S(2)}) async-start(), calls=%async_computation | async-start | bytes 15728640 | tf_op jit(solution)/shard_map/psum | solution.py:87
  6.5 14.9 %copy-start.2 = (bf16[3,512,1280]{2,1,0:T(8,128)(2,1)S(1)}, bf16[3,512,1280]{2,1,0:T(8,128)(2,1)}, u32[]{:S(2)}) copy-start(bf16[3,512,1280]{2,1,0:T(8,128)(2,1)} %param.6) | copy-start | bytes 11796484
  10.1 89.9 %collective-permute-start = (bf16[2,512,1280]{2,1,0:T(8,128)(2,1)}, bf16[2,512,1280]{2,1,0:T(8,128)(2,1)}, u32[]{:S(2)}, u32[]{:S(2)}) collective-permute-start(bf16[2,512,1280]{2,1,0:T(8,128)(2,1)} %slice.31), channel_id=1, source_target_pairs={{0,8},{4,12},{8,16},{12,20},{16,24},{20,28},{1,9},{5,13},{9,17},{1... | collective-permute-start | bytes 7864328 | tf_op jit(solution)/shard_map/ppermute | solution.py:15
  16.5 83.5 %collective-permute-start.1 = (bf16[2,512,1280]{2,1,0:T(8,128)(2,1)}, bf16[2,512,1280]{2,1,0:T(8,128)(2,1)}, u32[]{:S(2)}, u32[]{:S(2)}) collective-permute-start(bf16[2,512,1280]{2,1,0:T(8,128)(2,1)} %slice.31), channel_id=1, source_target_pairs={{0,4},{4,8},{8,12},{12,16},{16,20},{20,24},{24,28},{1,5},{5,9},{9,... | collective-permute-start | bytes 7864328 | tf_op jit(solution)/shard_map/ppermute | solution.py:15
  28.7 3.7 copy-start.7
  28.7 3.7 copy-start.8
  28.7 3.8 copy-start.10
  41.2 1.7 copy-start.3
  191.4 185.4 %copy-start = (bf16[2,640,1024]{1,2,0:T(8,128)(2,1)S(1)}, bf16[2,640,1024]{1,2,0:T(8,128)(2,1)}, u32[]{:S(2)}) copy-start(bf16[2,640,1024]{1,2,0:T(8,128)(2,1)} %copy.19) | copy-start | bytes 7864324
  376.8 4.0 %copy-start.1 = (f32[2,640,1024]{1,2,0:T(8,128)S(1)}, f32[2,640,1024]{1,2,0:T(8,128)}, u32[]{:S(2)}) copy-start(f32[2,640,1024]{1,2,0:T(8,128)} %get-tuple-element.82) | copy-start | bytes 15728644
  376.9 4.4 %copy-start.4 = (bf16[512,1280]{0,1:T(8,128)(2,1)S(1)}, bf16[512,1280]{0,1:T(8,128)(2,1)}, u32[]{:S(2)}) copy-start(bf16[512,1280]{0,1:T(8,128)(2,1)} %get-tuple-element.181) | copy-start | bytes 3932164
  381.3 2.0 copy-start.6
  381.3 2.1 copy-start.9
  383.4 1.7 copy-start.5
Sparse Core Ops, SparseCore 0:
  41.3 332.6 all-reduce.2
where the time goes:
time: 395 us; the launch traced here: 394 us
  waiting for transfers between devices  235 us (59%)
  matrix products  76 us (19%)
  other arithmetic  28.2 us (7%)
  local copies, waits for them, and re-layouts  23.8 us (6%)
  between operations  13.5 us (3%)
  starting transfers between devices  11.4 us (3%)
  loops' own time  6.39 us (2%)
    psum x1, waiting for transfers between devices, local(): grad_in, grad_out = lax.psum((grad_in, grad_out), 'ctx')  183 us
    ppermute x2, waiting for transfers between devices, shifted(): return lax.ppermute(array, axis, pairs)  52 us
    dot_general x10, matrix products, one_head(): return jnp.dot(probs_bf, window_head[1], preferred_element_type=jnp.float32)  37.4 us
    dot_general x10, matrix products, one_head(): jnp.dot(query_head, window_head[0].T, preferred_element_type=jnp.float32)  23 us
    reduce_sum x10, other arithmetic, one_head(): row_total = jnp.sum(weights, axis=-1, keepdims=True)  11.7 us
    ppermute x2, starting transfers between devices, shifted(): return lax.ppermute(array, axis, pairs)  11.4 us
    unnamed x25, local copies, waits for them, and re-layouts  8.62 us
  transfers between devices with their start and end apart: 3, of which 2 were waited for; matrix products, arithmetic and copies ran while one was open for 28% of the time, Pallas kernels for 0%

commit v1 on v0

v1 whole, which is shorter than its diff:
```python
import math

import jax
import jax.numpy as jnp
from jax import lax
from jax.experimental import pallas as pl
from jax.experimental.pallas import tpu as pltpu
from jax.sharding import PartitionSpec as P


ADIM = 128
EPS = 1e-06
F32 = jnp.float32
BF16 = jnp.bfloat16
PIECES = 4
VMEM_LIMIT = 20 * 1024 * 1024


VM = pl.BlockSpec(memory_space=pltpu.VMEM)
SM = pl.BlockSpec(memory_space=pltpu.SMEM)
HBM = pl.BlockSpec(memory_space=pltpu.HBM)


def sds(shape, dtype):
    return jax.ShapeDtypeStruct(shape, dtype)


def call(body, ins, outs, args, out_specs=None, scratch=()):
    return pl.pallas_call(
        body,
        in_specs=ins,
        out_specs=out_specs if out_specs is not None else [VM] * len(outs),
        out_shape=outs,
        scratch_shapes=list(scratch),
        compiler_params=pltpu.CompilerParams(vmem_limit_bytes=VMEM_LIMIT),
    )(*args)


def dot(a, b, dims):
    return lax.dot_general(a, b, (dims, ((), ())), preferred_element_type=F32)


def cut_blocks(info, qkv, picks, width):
    rows = qkv.shape[1]
    count = len(picks)

    def body(info_ref, qkv_ref, *rest):
        outs, sem = rest[:count], rest[count]
        copies = []
        for at, (which, own) in enumerate(picks):
            side = info_ref[0] if own else 1 - info_ref[0]
            cols = pl.ds(pl.multiple_of(side * width, ADIM), width)
            for piece in range(PIECES):
                some = pl.ds(piece * (rows // PIECES), rows // PIECES)
                copies.append(
                    pltpu.make_async_copy(
                        qkv_ref.at[which, some, cols], outs[at].at[some, :], sem.at[at, piece]
                    )
                )
        for copy in copies:
            copy.start()
        for copy in copies:
            copy.wait()

    return call(
        body,
        [SM, HBM],
        [sds((rows, width), BF16)] * count,
        (info, qkv),
        scratch=[pltpu.SemaphoreType.DMA((count, PIECES))],
    )


def stack_columns(arrays, cuts):
    count = len(arrays)

    def body(*refs):
        for (lo, hi), out in zip(cuts, refs[count:]):
            for at, ref in enumerate(refs[:count]):
                out[at] = ref[:, lo:hi]

    shapes = [(count, arrays[0].shape[0], hi - lo) for lo, hi in cuts]
    return call(body, [VM] * count, [sds(shape, BF16) for shape in shapes], arrays)


def gate_parts(keys, w_in, hidden_dim):
    projected = dot(keys, w_in, ((1,), (0,)))
    gate = projected[:, :hidden_dim]
    up = projected[:, hidden_dim:]
    sig = jax.nn.sigmoid(gate)
    act = gate * sig
    slope = sig * (1.0 + gate * (1.0 - sig))
    return (act * up).astype(BF16), up * slope, act


def scale_rows(vals, rate_rows):
    return (jnp.transpose(rate_rows)[:, :1] * vals.astype(F32)).astype(BF16)


def back_parts(scaled, w_out, tilt, act):
    back = dot(scaled, w_out, ((1,), (1,)))
    return (back * tilt).astype(BF16), (back * act).astype(BF16)


def grads_own(info, keys, vals, rates, fast_in, fast_out):
    width = keys.shape[1]
    hidden_dim = fast_out.shape[1]

    def body(info_ref, k_ref, v_ref, rate_ref, win_ref, wout_ref, gin_ref, gout_ref):
        keep = info_ref[0]
        hidden, tilt, act = gate_parts(k_ref[...], win_ref[keep], hidden_dim)
        scaled = scale_rows(v_ref[...], rate_ref[...])
        pre_gate, pre_up = back_parts(scaled, wout_ref[keep], tilt, act)
        gin_ref[:, :hidden_dim] = dot(k_ref[...], pre_gate, ((0,), (0,)))
        gin_ref[:, hidden_dim:] = dot(k_ref[...], pre_up, ((0,), (0,)))
        gout_ref[...] = dot(hidden, scaled, ((0,), (0,)))

    return call(
        body,
        [SM] + [VM] * 5,
        [sds((width, 2 * hidden_dim), F32), sds((hidden_dim, width), F32)],
        (info, keys, vals, rates, fast_in, fast_out),
    )


def pair_gates(info, keys, fast_in, hidden_dim):
    rows = keys.shape[0]

    def body(info_ref, k_ref, win_ref, hid_ref, tilt_ref, act_ref):
        hidden, tilt, act = gate_parts(k_ref[...], win_ref[info_ref[0]], hidden_dim)
        hid_ref[...] = hidden
        tilt_ref[...] = tilt
        act_ref[...] = act

    shape = (rows, hidden_dim)
    return call(
        body,
        [SM, VM, VM],
        [sds(shape, BF16), sds(shape, F32), sds(shape, F32)],
        (info, keys, fast_in),
    )


def pair_first(hidden, vals, rates, gout, lo, hi):
    def body(h_ref, v_ref, rate_ref, gout_ref, scaled_ref, send_ref, kept_ref):
        scaled = scale_rows(v_ref[...], rate_ref[...])
        scaled_ref[...] = scaled
        part = gout_ref[:, lo:hi] + dot(h_ref[...], scaled[:, lo:hi], ((0,), (0,)))
        send_ref[...] = part.astype(BF16)
        kept_ref[...] = part

    shape = (gout.shape[0], hi - lo)
    return call(
        body,
        [VM] * 4,
        [sds(vals.shape, BF16), sds(shape, BF16), sds(shape, F32)],
        (hidden, vals, rates, gout),
    )


def pair_grads(info, keys, scaled, fast_out, gates, gin, gout, in_cuts, out_cuts):
    width = keys.shape[1]
    hidden_dim = fast_out.shape[1]
    count = len(in_cuts) + len(out_cuts)

    def body(info_ref, k_ref, s_ref, wout_ref, h_ref, t_ref, a_ref, gin_ref, gout_ref, *o):
        pre_gate, pre_up = back_parts(s_ref[...], wout_ref[info_ref[0]], t_ref[...], a_ref[...])
        for at, (lo, hi) in enumerate(in_cuts):
            size = hi - lo
            for start, base, pre in ((0, lo, pre_gate), (size, hidden_dim + lo, pre_up)):
                part = gin_ref[:, base : base + size]
                part += dot(k_ref[...], pre[:, lo:hi], ((0,), (0,)))
                o[at][:, start : start + size] = part.astype(BF16)
                o[count + at][:, start : start + size] = part
        for at, (lo, hi) in enumerate(out_cuts, len(in_cuts)):
            part = gout_ref[:, lo:hi] + dot(h_ref[...], s_ref[:, lo:hi], ((0,), (0,)))
            o[at][...] = part.astype(BF16)
            o[count + at][...] = part

    shapes = [(width, 2 * (hi - lo)) for lo, hi in in_cuts]
    shapes += [(hidden_dim, hi - lo) for lo, hi in out_cuts]
    outs = call(
        body,
        [SM] + [VM] * 8,
        [sds(s, BF16) for s in shapes] + [sds(s, F32) for s in shapes],
        (info, keys, scaled, fast_out, *gates, gin, gout),
    )
    return outs[:count], outs[count:]


def add_chunk(kept, got):
    def body(kept_ref, got_ref, send_ref, sum_ref):
        total = kept_ref[...] + got_ref[...].astype(F32)
        send_ref[...] = total.astype(BF16)
        sum_ref[...] = total

    return call(body, [VM] * 2, [sds(kept.shape, BF16), sds(kept.shape, F32)], (kept, got))


def new_weights(info, mine, others, fast, lo, hi, factor, paired):
    count = len(others)
    size = hi - lo
    half = fast.shape[2] // 2

    def body(info_ref, a_ref, *rest):
        w_ref, o_ref = rest[count:]
        keep = info_ref[0]
        spans = [(0, lo)] + ([(size, half + lo)] if paired else [])
        for start, col in spans:
            total = a_ref[:, start : start + size]
            for b_ref in rest[:count]:
                total += b_ref[:, start : start + size].astype(F32)
            old = w_ref[keep, :, col : col + size].astype(F32)
            moved = old + total * factor
            old_norm = jnp.sqrt(jnp.sum(old * old, axis=0, keepdims=True))
            new_norm = jnp.sqrt(jnp.sum(moved * moved, axis=0, keepdims=True))
            o_ref[:, start : start + size] = (moved * (old_norm / (new_norm + EPS))).astype(BF16)

    return call(
        body, [SM] + [VM] * (count + 2), [sds(mine.shape, BF16)], (info, mine, *others, fast)
    )[0]


def query_hidden(info, q_own, q_oth, made, got):
    rows = q_own.shape[0]
    size = made.shape[1] // 2

    def body(info_ref, qa_ref, qb_ref, made_ref, got_ref, o_ref):
        def run(w_ref):
            for start, ref in ((0, qa_ref), (rows, qb_ref)):
                proj = dot(ref[...], w_ref[...], ((1,), (0,)))
                gate = proj[:, :size]
                o_ref[start : start + rows, :] = (
                    gate * jax.nn.sigmoid(gate) * proj[:, size:]
                ).astype(BF16)

        @pl.when(info_ref[2] == 1)
        def _():
            run(made_ref)

        @pl.when(info_ref[2] != 1)
        def _():
            run(got_ref)

    return call(
        body, [SM] + [VM] * 4, [sds((2 * rows, size), BF16)], (info, q_own, q_oth, made, got)
    )[0]


def apply_chunk(info, hiddens, made, got, parts, late, lo, hi):
    rows = hiddens[0].shape[0] // 2
    size = hi - lo
    count = len(hiddens)
    (own_sum, own_at, own_p), (oth_sum, oth_at, oth_p) = parts
    vals = [array for group in late for array, _, _ in group]

    def body(info_ref, *refs):
        hid = refs[:count]
        made_ref, got_ref = refs[count : count + 2]
        val_refs = list(refs[count + 2 : count + 2 + len(vals)])
        att = refs[count + 2 + len(vals) : -2]
        own_ref, oth_ref = refs[-2:]
        groups = [[(val_refs.pop(0), *place) for _, *place in group] for group in late]

        def values(group, head):
            total = None
            for ref, base, layer_at in group:
                col = lo - base + head * ADIM
                cols = slice(col, col + ADIM)
                piece = ref[:, cols] if layer_at is None else ref[layer_at, :, cols]
                total = piece if total is None else total + piece
            return total

        def run(w_ref):
            for start, out, sum_ref, base, p_ref, order in (
                (rows, oth_ref, att[2], oth_at, att[3], (1, 0)),
                (0, own_ref, att[0], own_at, att[1], (0, 1)),
            ):
                total = sum_ref[:, base : base + size]
                row = 0
                for ref in hid:
                    part = ref.shape[1]
                    total += dot(
                        ref[start : start + rows, :], w_ref[row : row + part, :], ((1,), (0,))
                    )
                    row += part
                for head in range(size // ADIM):
                    col = head * ADIM
                    mixed = total[:, col : col + ADIM]
                    for place, which in enumerate(order):
                        p = p_ref[base // ADIM + head, :, place * rows : (place + 1) * rows]
                        v = values(groups[which], head)
                        if place == 1:
                            v = jnp.where(info_ref[0] == which, jnp.zeros_like(v), v)
                        mixed += dot(p, v, ((1,), (0,)))
                    out[:, col : col + ADIM] = mixed.astype(BF16)

        @pl.when(info_ref[2] == 1)
        def _():
            run(made_ref)

        @pl.when(info_ref[2] != 1)
        def _():
            run(got_ref)

    return call(
        body,
        [SM] + [VM] * (count + 2 + len(vals) + 4),
        [sds((rows, size), BF16)] * 2,
        (info, *hiddens, made, got, *vals, own_sum, own_p, oth_sum, oth_p),
    )


def attention(info, side, heads, q, k_own, v_own, k_oth, v_oth, pk_own, pk_oth):
    rows = q.shape[0]
    tile = min(256, rows)
    first, last = heads
    number = last - first
    scale = ADIM ** (-0.5) * math.log2(math.e)
    if side == 0:
        arrays = (q, k_own, v_own, pk_own, k_oth, v_oth, pk_oth)
    else:
        arrays = (q, k_oth, v_oth, pk_oth, k_own, v_own, pk_own)

    def body(info_ref, q_ref, kc, vc, kp, k_pair, v_pair, k_before, o_ref, p_ref, kf, vf):
        has_prev = info_ref[1] > 0
        in_pair = info_ref[0] == 1 - side
        row = lax.broadcasted_iota(jnp.int32, (tile, tile), 0)
        col = lax.broadcasted_iota(jnp.int32, (tile, tile), 1)
        causal = col <= row
        prev_floor = jnp.where(has_prev, 0.0, -1e30)
        full_floor = jnp.where(jnp.logical_or(in_pair, has_prev), 0.0, -1e30)

        def one_head(at, carry):
            cols = pl.ds(pl.multiple_of((first + at) * ADIM, ADIM), ADIM)
            outs = pl.ds(pl.multiple_of(at * ADIM, ADIM), ADIM)

            @pl.when(in_pair)
            def _():
                kf[...] = k_pair[:, cols]
                vf[...] = v_pair[:, cols]

            @pl.when(jnp.logical_not(in_pair))
            def _():
                kf[...] = k_before[:, cols]
                vf[...] = jnp.zeros_like(vf)

            for t in range(rows // tile):
                lo, hi = t * tile, (t + 1) * tile
                qt = q_ref[lo:hi, cols]
                s_cur = dot(qt, kc[0:hi, cols], ((1,), (1,)))
                s_prev = dot(qt, kp[lo:, cols], ((1,), (1,))) + prev_floor
                s_full = dot(qt, kf[...], ((1,), (1,))) + full_floor
                s_rest = [jnp.where(causal, s_cur[:, lo:hi], s_prev[:, :tile]), s_full]
                if lo:
                    s_rest.append(s_cur[:, :lo])
                if hi < rows:
                    s_rest.append(s_prev[:, tile:])
                top = s_rest[0].max(axis=1, keepdims=True)
                for s in s_rest[1:]:
                    top = jnp.maximum(top, s.max(axis=1, keepdims=True))
                es = [jnp.exp2((s - top) * scale) for s in s_rest]
                total = es[0].sum(axis=1, keepdims=True)
                for e in es[1:]:
                    total += e.sum(axis=1, keepdims=True)
                share = 1.0 / total
                e_cur = jnp.where(causal, es[0], 0.0).astype(BF16)
                acc = dot(e_cur, vc[lo:hi, cols], ((1,), (0,)))
                acc += dot(es[1].astype(BF16), vf[...], ((1,), (0,)))
                if lo:
                    acc += dot(es[2].astype(BF16), vc[:lo, cols], ((1,), (0,)))
                    p_ref[at, lo:hi, :lo] = jnp.zeros((tile, lo), BF16)
                p_ref[at, lo:hi, lo:hi] = jnp.where(causal, 0.0, es[0] * share).astype(BF16)
                if hi < rows:
                    p_ref[at, lo:hi, hi:rows] = (es[-1] * share).astype(BF16)
                p_ref[at, lo:hi, rows:] = (es[1] * share).astype(BF16)
                o_ref[lo:hi, outs] = acc * share
            return carry

        lax.fori_loop(0, number, one_head, 0)

    return call(
        body,
        [SM] + [VM] * 7,
        [sds((rows, number * ADIM), F32), sds((number, rows, 2 * rows), BF16)],
        (info, *arrays),
        scratch=[pltpu.VMEM((rows, ADIM), BF16)] * 2,
    )


def assemble(info, own_parts, oth_parts, cuts):
    rows = own_parts[0].shape[0]
    width = cuts[-1][1]
    count = len(cuts)

    def body(info_ref, *refs):
        parts, out, sem = refs[: 2 * count], refs[2 * count], refs[2 * count + 1]
        copies = []
        for at, ref in enumerate(parts):
            side = info_ref[0] if at < count else 1 - info_ref[0]
            lo, hi = cuts[at % count]
            start = pl.multiple_of(side * width + lo, ADIM)
            copies.append(
                pltpu.make_async_copy(ref, out.at[:, pl.ds(start, hi - lo)], sem.at[at])
            )
        for copy in copies:
            copy.start()
        for copy in copies:
            copy.wait()

    return call(
        body,
        [SM] + [VM] * (2 * count),
        [sds((rows, 2 * width), BF16)],
        (info, *own_parts, *oth_parts),
        out_specs=[HBM],
        scratch=[pltpu.SemaphoreType.DMA((2 * count,))],
    )[0]


def rate_rows(info, step_size):
    rows = step_size.shape[0]

    def body(info_ref, step_ref, own_ref, send_ref):
        both = jnp.transpose(step_ref[...])
        upper = info_ref[0] == 1
        own_ref[...] = jnp.broadcast_to(jnp.where(upper, both[1:2], both[0:1]), (8, rows))
        send_ref[...] = jnp.broadcast_to(jnp.where(upper, both[0:1], both[1:2]), (8, rows))

    return call(body, [SM, VM], [sds((8, rows), F32)] * 2, (info, step_size))


def layer(qkv, step_size, fast_in, fast_out):
    _, tok_rows, _ = qkv.shape
    head_width = fast_in.shape[1]
    hidden_dim = fast_out.shape[1]
    ctx_count = lax.axis_size("ctx")
    line = ctx_count // 2
    index = lax.axis_index("ctx").astype(jnp.int32)
    keep = index % 2
    place = index // 2
    inner = ((place == line // 2) | (place == line // 2 - 1)).astype(jnp.int32)
    info = jnp.stack([keep, place, inner])
    factor = (tok_rows * ctx_count) ** (-0.5)

    swap_pairs = [(i, i ^ 1) for i in range(ctx_count)]
    next_pairs = [(i, i + 2) for i in range(ctx_count - 2)]

    def along(moves):
        return [(2 * a + y, 2 * b + y) for a, b in moves for y in (0, 1)]

    def permute(array, pairs):
        return lax.ppermute(array, "ctx", pairs)

    parts = 4
    part = hidden_dim // parts
    in_cuts = [(i * part, (i + 1) * part) for i in range(parts)]
    middle = (head_width // ADIM + 1) // 2 * ADIM
    out_cuts = [(0, middle), (middle, head_width)]

    qkv = pltpu.with_memory_space_constraint(qkv, pltpu.HBM)
    k_away, k_own = cut_blocks(info, qkv, [(1, False), (1, True)], head_width)
    k_oth = permute(k_away, swap_pairs)
    pk_own = permute(k_own, next_pairs)
    v_away, v_own = cut_blocks(info, qkv, [(2, False), (2, True)], head_width)
    rate_own, rate_send = rate_rows(info, step_size)
    rate_oth = permute(rate_send, swap_pairs)
    v_oth = permute(v_away, swap_pairs)
    q_away, q_own = cut_blocks(info, qkv, [(0, False), (0, True)], head_width)
    q_oth = permute(q_away, swap_pairs)
    pk_oth = permute(k_oth, next_pairs)
    if line == 4:
        own_early = permute(v_own, along([(1, 2), (2, 3)]))
        oth_early = permute(v_oth, along([(2, 3)]))
        stacks = stack_columns((v_own, v_oth), out_cuts)
        singles = stack_columns((v_oth,), out_cuts)
        late_vals = []
        for i, (lo, hi) in enumerate(out_cuts):
            first = permute(stacks[i], along([(0, 1)]))
            second = permute(singles[i], along([(1, 2)]))
            late_vals.append((
                [(own_early, 0, None), (first, lo, 0)],
                [(oth_early, 0, None), (first, lo, 1), (second, lo, 0)],
            ))
    else:
        late_vals = [(
            [(permute(v_own, next_pairs), 0, None)], [(permute(v_oth, next_pairs), 0, None)]
        )] * len(out_cuts)

    gin, gout = grads_own(info, k_own, v_own, rate_own, fast_in, fast_out)
    gates = pair_gates(info, k_oth, fast_in, hidden_dim)
    scaled, *first = pair_first(gates[0], v_oth, rate_oth, gout, *out_cuts[0])
    send, kept = pair_grads(
        info, k_oth, scaled, fast_out, gates, gin, gout, in_cuts, out_cuts[1:]
    )
    send, kept = [first[0], *send], [first[1], *kept]
    plan = [(fast_out, *out_cuts[0], False)]
    plan += [(fast_in, lo, hi, True) for lo, hi in in_cuts]
    plan += [(fast_out, lo, hi, False) for lo, hi in out_cuts[1:]]

    made, got = [], []
    if line == 4:
        inward = along([(0, 1), (3, 2)])
        centre = along([(1, 2), (2, 1)])
        outward = along([(1, 0), (2, 3)])
        for at, (fast, lo, hi, paired) in enumerate(plan):
            half_sum, total = add_chunk(kept[at], permute(send[at], inward))
            crossed = [permute(half_sum, centre)]
            made.append(new_weights(info, total, crossed, fast, lo, hi, factor, paired))
            got.append(permute(made[at], outward))
    else:
        for at, (fast, lo, hi, paired) in enumerate(plan):
            slots = jnp.where(jnp.arange(2)[:, None, None] == keep, kept[at][None], 0.0)
            total = lax.dynamic_index_in_dim(lax.psum(slots, "ctx"), keep, 0, keepdims=False)
            made.append(new_weights(info, total, (), fast, lo, hi, factor, paired))
        got = made

    heads = head_width // ADIM
    split = middle // ADIM
    blocks = (k_own, v_own, k_oth, v_oth, pk_own, pk_oth)
    own_sum, own_p = attention(info, 0, (0, heads), q_own, *blocks)
    oth_some = attention(info, 1, (0, split), q_oth, *blocks)
    oth_rest = attention(info, 1, (split, heads), q_oth, *blocks)
    hiddens = [query_hidden(info, q_own, q_oth, made[i], got[i]) for i in range(1, 1 + parts)]
    own_parts, oth_parts = [], []
    for i, (lo, hi) in enumerate(out_cuts):
        at = parts + i if i else 0
        left = (own_sum, lo, own_p), (
            (oth_some[0], lo, oth_some[1]) if lo < middle else (oth_rest[0], lo - middle, oth_rest[1])
        )
        mine, theirs = apply_chunk(info, hiddens, made[at], got[at], left, late_vals[i], lo, hi)
        own_parts.append(mine)
        oth_parts.append(permute(theirs, swap_pairs))
    return assemble(info, own_parts, oth_parts, out_cuts)


def solution(mesh):
    placed = (
        P(None, "ctx", "head"),
        P("ctx", "head"),
        P("head", None, None),
        P("head", None, None),
    )
    return jax.shard_map(
        layer, mesh=mesh, in_specs=placed, out_specs=P("ctx", "head"), check_vma=False
    )
```

time: 395 us -> 210 us (0.53)
  waiting for transfers between devices: 235 us -> 72 us
  matrix products: 76 us -> 0 us
  starting transfers between devices: 11.4 us -> 72.3 us
  Pallas kernels: 0 us -> 60.6 us
  other arithmetic: 28.2 us -> 0.08 us
  local copies, waits for them, and re-layouts: 23.8 us -> 2.32 us
  between operations: 13.5 us -> 0.81 us
  loops' own time: 6.39 us -> 0 us
    psum x1 -> x0, waiting for transfers between devices: 183 us -> none  [local(): grad_in, grad_out = lax.psum((grad_in, grad_out), 'ctx')]
    dot_general x26 -> x0, matrix products: 76 us -> none  [the longest x10 37.4 us: one_head(): return jnp.dot(probs_bf, window_head[1], preferred_element_type=jnp.float32)]
    ppermute x2 -> x32, starting transfers between devices: 11.4 us -> 72.3 us  [permute(): return lax.ppermute(array, 'ctx', pairs)]
    pallas_call x0 -> x32, Pallas kernels: none -> 60.6 us  [call(): pl.pallas_call(body, in_specs=ins, out_specs=out_specs if out_specs is no...]
    ppermute x2 -> x32, waiting for transfers between devices: 52 us -> 72 us  [permute(): return lax.ppermute(array, 'ctx', pairs)]
    reduce_sum x12 -> x0, other arithmetic: 18.4 us -> none  [the longest x10 11.7 us: one_head(): row_total = jnp.sum(weights, axis=-1, keepdims=True)]
    concatenate x1 -> x0, other arithmetic: 6.96 us -> none  [local(): window_pair = jnp.concatenate([far_pair, near_pair, own_pair], axis=1)]
    another operation x1 -> x0, loops' own time: 6.39 us -> none  [local(): attended = lax.map(one_head, jnp.arange(head_count, dtype=jnp.int32))]
  transfers between devices with their start and end apart: 3 -> 32, of which waited for: 2 -> 12; matrix products, arithmetic and copies ran while one was open for 28% -> 0% of each run, Pallas kernels for 0% -> 27%
where the time goes in v1:
time: 210 us; the launch traced here: 208 us
  starting transfers between devices  72.3 us (34%)
  waiting for transfers between devices  72 us (34%)
  Pallas kernels  60.6 us (29%)
  local copies, waits for them, and re-layouts  2.32 us (1%)
    ppermute x32, starting transfers between devices, permute(): return lax.ppermute(array, 'ctx', pairs)  72.3 us
    ppermute x32, waiting for transfers between devices, permute(): return lax.ppermute(array, 'ctx', pairs)  72 us
    pallas_call x32, Pallas kernels, call(): pl.pallas_call(body, in_specs=ins, out_specs=out_specs if out_specs is no...  60.6 us
  transfers between devices with their start and end apart: 32, of which 12 were waited for; matrix products, arithmetic and copies ran while one was open for 0% of the time, Pallas kernels for 27%

profile of v1, /device:TPU:0, one launch (start us, length us, event | category | flops | bytes accessed | tf_op | source)
XLA Modules:
  0.0 208.1 jit_solution(15154371123030589969)
XLA Ops:
  0.1 3.1 %shard_map.47 = (bf16[512,640]{1,0:T(8,128)(2,1)}, bf16[512,640]{1,0:T(8,128)(2,1)}) custom-call(s32[3]{0:T(128)S(1)} %pad_add_fusion.info_ref, bf16[3,512,1280]{2,1,0:T(8,128)(2,1)} %qkv_ref.5), custom_call_target="tpu_custom_call" | custom-call | tf_op jit(solution)/shard_map/pallas_call | solution.py:29
  3.2 3.1 %collective-permute-start.1 = (bf16[512,640]{1,0:T(8,128)(2,1)}, bf16[512,640]{1,0:T(8,128)(2,1)}, u32[]{:S(2)}, u32[]{:S(2)}) collective-permute-start(bf16[512,640]{1,0:T(8,128)(2,1)} %get-tuple-element.59), channel_id=1, source_target_pairs={{0,4},{4,0},{8,12},{12,8},{16,20},{20,16},{24,28},{28,24},{1,5},{5... | collective-permute-start | bytes 1966088 | tf_op jit(solution)/shard_map/ppermute | solution.py:453
  6.2 3.1 %shard_map.49 = (bf16[512,640]{1,0:T(8,128)(2,1)}, bf16[512,640]{1,0:T(8,128)(2,1)}) custom-call(s32[3]{0:T(128)S(1)} %pad_add_fusion.info_ref, bf16[3,512,1280]{2,1,0:T(8,128)(2,1)} %qkv_ref.5), custom_call_target="tpu_custom_call" | custom-call | tf_op jit(solution)/shard_map/pallas_call | solution.py:29
  9.4 3.0 %shard_map.46 = (bf16[512,640]{1,0:T(8,128)(2,1)}, bf16[512,640]{1,0:T(8,128)(2,1)S(1)}) custom-call(s32[3]{0:T(128)S(1)} %pad_add_fusion.info_ref, bf16[3,512,1280]{2,1,0:T(8,128)(2,1)} %qkv_ref.5), custom_call_target="tpu_custom_call" | custom-call | tf_op jit(solution)/shard_map/pallas_call | solution.py:29
  13.3 1.9 collective-permute-start
  15.1 4.3 %collective-permute-start.23 = (bf16[512,640]{1,0:T(8,128)(2,1)}, bf16[512,640]{1,0:T(8,128)(2,1)}, u32[]{:S(2)}, u32[]{:S(2)}) collective-permute-start(bf16[512,640]{1,0:T(8,128)(2,1)} %get-tuple-element.63.k_ref.kc.k_pair), channel_id=1, source_target_pairs={{0,8},{4,12},{8,16},{12,20},{16,24},{20,28},{1,9},{5,13},{9,17},{1... | collective-permute-start | bytes 1966088 | tf_op jit(solution)/shard_map/ppermute | solution.py:453
  22.1 2.0 collective-permute-start.3
  25.5 4.0 %shard_map.51 = (f32[640,1024]{1,0:T(8,128)S(1)}, f32[512,640]{1,0:T(8,128)S(1)}) custom-call(s32[3]{0:T(128)S(1)} %pad_add_fusion.info_ref, bf16[512,640]{1,0:T(8,128)(2,1)} %get-tuple-element.63.k_ref.kc.k_pair, bf16[512,640]{1,0:T(8,128)(2,1)} %get-tuple-element.64.v_ref.refs_0_.vc.v_pair, f32[8,512]{1,0:T(8,128)S(1)} %get-tuple-element.65.rate_ref, ...), custom_call_target="tpu_custom_call" | custom-call | tf_op jit(solution)/shard_map/pallas_call | solution.py:29
  29.4 2.3 %shard_map.48 = (bf16[512,512]{1,0:T(8,128)(2,1)S(1)}, f32[512,512]{1,0:T(8,128)S(1)}, f32[512,512]{1,0:T(8,128)S(1)}) custom-call(s32[3]{0:T(128)S(1)} %pad_add_fusion.info_ref, bf16[512,640]{1,0:T(8,128)(2,1)} %collective-permute-done.1.k_ref.k_pair.kc, bf16[2,640,1024]{2,1,0:T(8,128)(2,1)S(1)} %copy-done), custom_call_target="tpu_custom_call" | custom-call | tf_op jit(solution)/shard_map/pallas_call | solution.py:29
  31.8 17.8 %collective-permute-done.3.rate_ref = f32[8,512]{1,0:T(8,128)S(1)} collective-permute-done((f32[8,512]{1,0:T(8,128)S(1)}, f32[8,512]{1,0:T(8,128)S(1)}, u32[]{:S(2)}, u32[]{:S(2)}) %collective-permute-start.3) | collective-permute-done | bytes 16416 | tf_op jit(solution)/shard_map/ppermute | solution.py:453
  49.6 1.8 shard_map.52
  51.5 3.4 %shard_map.53 = (bf16[640,256]{1,0:T(8,128)(2,1)S(1)}, bf16[640,256]{1,0:T(8,128)(2,1)S(1)}, bf16[640,256]{1,0:T(8,128)(2,1)S(1)}, bf16[640,256]{1,0:T(8,128)(2,...) custom-call(s32[3]{0:T(128)S(1)} %pad_add_fusion.info_ref, ...), custom_call_target="tpu_custom_call" | custom-call | tf_op jit(solution)/shard_map/pallas_call | solution.py:29
  54.9 3.7 %collective-permute-start.13 = (bf16[640,256]{1,0:T(8,128)(2,1)S(1)}, bf16[640,256]{1,0:T(8,128)(2,1)S(1)}, u32[]{:S(2)}, u32[]{:S(2)}) collective-permute-start(bf16[640,256]{1,0:T(8,128)(2,1)S(1)} %get-tuple-element.84), channel_id=1, source_target_pairs={{0,8},{4,12},{24,16},{28,20},{1,9},{5,13},{25,17},{29,21},{2,10},{... | collective-permute-start | bytes 983048 | tf_op jit(solution)/shard_map/ppermute | solution.py:453
  63.9 8.4 %collective-permute-done.25.got_ref = bf16[512,256]{1,0:T(8,128)(2,1)S(1)} collective-permute-done((bf16[512,256]{1,0:T(8,128)(2,1)S(1)}, bf16[512,256]{1,0:T(8,128)(2,1)S(1)}, u32[]{:S(2)}, u32[]{:S(2)}) %collective-permute-start.25) | collective-permute-done | bytes 262176 | tf_op jit(solution)/shard_map/ppermute | solution.py:453
  72.3 4.4 %collective-permute-start.16 = (bf16[512,384]{1,0:T(8,128)(2,1)S(1)}, bf16[512,384]{1,0:T(8,128)(2,1)S(1)}, u32[]{:S(2)}, u32[]{:S(2)}) collective-permute-start(bf16[512,384]{1,0:T(8,128)(2,1)S(1)} %get-tuple-element.88), channel_id=1, source_target_pairs={{0,8},{4,12},{24,16},{28,20},{1,9},{5,13},{25,17},{29,21},{2,10},{... | collective-permute-start | bytes 1179656 | tf_op jit(solution)/shard_map/ppermute | solution.py:453
  80.0 6.3 %collective-permute-done.7.got_ref = bf16[640,256]{1,0:T(8,128)(2,1)S(1)} collective-permute-done((bf16[640,256]{1,0:T(8,128)(2,1)S(1)}, bf16[640,256]{1,0:T(8,128)(2,1)S(1)}, u32[]{:S(2)}, u32[]{:S(2)}) %collective-permute-start.7) | collective-permute-done | bytes 327712 | tf_op jit(solution)/shard_map/ppermute | solution.py:453
  87.0 6.3 %collective-permute-done.4.got_ref = bf16[640,256]{1,0:T(8,128)(2,1)S(1)} collective-permute-done((bf16[640,256]{1,0:T(8,128)(2,1)S(1)}, bf16[640,256]{1,0:T(8,128)(2,1)S(1)}, u32[]{:S(2)}, u32[]{:S(2)}) %collective-permute-start.4) | collective-permute-done | bytes 327712 | tf_op jit(solution)/shard_map/ppermute | solution.py:453
  93.4 4.4 %collective-permute-start.24 = (bf16[512,640]{1,0:T(8,128)(2,1)}, bf16[512,640]{1,0:T(8,128)(2,1)S(1)}, u32[]{:S(2)}, u32[]{:S(2)}) collective-permute-start(bf16[512,640]{1,0:T(8,128)(2,1)} %collective-permute-done.1.k_ref.k_pair.kc), channel_id=1, source_target_pairs={{0,8},{4,12},{8,16},{12,20},{16,24},{20,28},{1,9},{5,13},{9,17},{1... | collective-permute-start | bytes 1966088 | tf_op jit(solution)/shard_map/ppermute | solution.py:453
  97.9 3.9 %collective-permute-done.16.got_ref = bf16[512,384]{1,0:T(8,128)(2,1)S(1)} collective-permute-done((bf16[512,384]{1,0:T(8,128)(2,1)S(1)}, bf16[512,384]{1,0:T(8,128)(2,1)S(1)}, u32[]{:S(2)}, u32[]{:S(2)}) %collective-permute-start.16) | collective-permute-done | bytes 393248 | tf_op jit(solution)/shard_map/ppermute | solution.py:453
  106.9 24.0 %collective-permute-start.20 = (bf16[2,512,384]{2,1,0:T(8,128)(2,1)S(1)}, bf16[2,512,384]{2,1,0:T(8,128)(2,1)S(1)}, u32[]{:S(2)}, u32[]{:S(2)}) collective-permute-start(bf16[2,512,384]{2,1,0:T(8,128)(2,1)S(1)} %get-tuple-element.91), channel_id=1, source_target_pairs={{0,8},{4,12},{1,9},{5,13},{2,10},{6,14},{3,11},{7,15}} | collective-permute-start | bytes 2359304 | tf_op jit(solution)/shard_map/ppermute | solution.py:453
  140.5 5.4 %collective-permute-done.15.got_ref = bf16[640,256]{1,0:T(8,128)(2,1)S(1)} collective-permute-done((bf16[640,256]{1,0:T(8,128)(2,1)S(1)}, bf16[640,256]{1,0:T(8,128)(2,1)S(1)}, u32[]{:S(2)}, u32[]{:S(2)}) %collective-permute-start.15) | collective-permute-done | bytes 327712 | tf_op jit(solution)/shard_map/ppermute | solution.py:453
  147.2 5.7 %collective-permute-done.12.got_ref = bf16[640,256]{1,0:T(8,128)(2,1)S(1)} collective-permute-done((bf16[640,256]{1,0:T(8,128)(2,1)S(1)}, bf16[640,256]{1,0:T(8,128)(2,1)S(1)}, u32[]{:S(2)}, u32[]{:S(2)}) %collective-permute-start.12) | collective-permute-done | bytes 327712 | tf_op jit(solution)/shard_map/ppermute | solution.py:453
  155.1 4.8 %collective-permute-done.9.got_ref = bf16[640,256]{1,0:T(8,128)(2,1)S(1)} collective-permute-done((bf16[640,256]{1,0:T(8,128)(2,1)S(1)}, bf16[640,256]{1,0:T(8,128)(2,1)S(1)}, u32[]{:S(2)}, u32[]{:S(2)}) %collective-permute-start.9) | collective-permute-done | bytes 327712 | tf_op jit(solution)/shard_map/ppermute | solution.py:453
  160.6 6.3 %collective-permute-done.6.got_ref = bf16[640,256]{1,0:T(8,128)(2,1)S(1)} collective-permute-done((bf16[640,256]{1,0:T(8,128)(2,1)S(1)}, bf16[640,256]{1,0:T(8,128)(2,1)S(1)}, u32[]{:S(2)}, u32[]{:S(2)}) %collective-permute-start.6) | collective-permute-done | bytes 327712 | tf_op jit(solution)/shard_map/ppermute | solution.py:453
  168.4 8.1 %shard_map.70 = (f32[512,640]{1,0:T(8,128)S(1)}, bf16[5,512,1024]{2,1,0:T(8,128)(2,1)S(1)}) custom-call(s32[3]{0:T(128)S(1)} %pad_add_fusion.info_ref, bf16[512,640]{1,0:T(8,128)(2,1)S(1)} %copy-done.4, bf16[512,640]{1,0:T(8,128)(2,1)} %get-tuple-element.63.k_ref.kc.k_pair, bf16[512,640]{1,0:T(8,128)(2,1)} %get-tuple-element.64.v_ref.refs_0_.vc.v_pair, ...), custom_call_target="tpu_custom_call" | custom-call | tf_op jit(solution)/shard_map/pallas_call | solution.py:29
  176.5 5.7 %shard_map.71 = (f32[512,384]{1,0:T(8,128)S(1)}, bf16[3,512,1024]{2,1,0:T(8,128)(2,1)S(1)}) custom-call(s32[3]{0:T(128)S(1)} %pad_add_fusion.info_ref, bf16[512,640]{1,0:T(8,128)(2,1)S(1)} %collective-permute-done.qb_ref.q_ref, bf16[512,640]{1,0:T(8,128)(2,1)} %collective-permute-done.1.k_ref.k_pair.kc, ...), custom_call_target="tpu_custom_call" | custom-call | tf_op jit(solution)/shard_map/pallas_call | solution.py:29
  186.8 3.8 %shard_map.72 = (bf16[512,384]{1,0:T(8,128)(2,1)S(1)}, bf16[512,384]{1,0:T(8,128)(2,1)S(1)}) custom-call(s32[3]{0:T(128)S(1)} %pad_add_fusion.info_ref, bf16[1024,128]{1,0:T(8,128)(2,1)S(1)} %shard_map.56.refs_0_, bf16[1024,128]{1,0:T(8,128)(2,1)S(1)} %shard_map.59.refs_1_, bf16[1024,128]{1,0:T(8,128)(2,1)S(1)} %shard_map.62.refs_2_, ...), custom_call_target="tpu_custom_call" | custom-call | tf_op jit(solution)/shard_map/pallas_call | solution.py:29
  190.6 1.6 collective-permute-start.30
  192.2 4.4 %shard_map.75 = (f32[512,256]{1,0:T(8,128)S(1)}, bf16[2,512,1024]{2,1,0:T(8,128)(2,1)S(1)}) custom-call(s32[3]{0:T(128)S(1)} %pad_add_fusion.info_ref, bf16[512,640]{1,0:T(8,128)(2,1)S(1)} %collective-permute-done.qb_ref.q_ref, bf16[512,640]{1,0:T(8,128)(2,1)} %collective-permute-done.1.k_ref.k_pair.kc, ...), custom_call_target="tpu_custom_call" | custom-call | tf_op jit(solution)/shard_map/pallas_call | solution.py:29
  196.6 3.2 %shard_map.76 = (bf16[512,256]{1,0:T(8,128)(2,1)S(1)}, bf16[512,256]{1,0:T(8,128)(2,1)S(1)}) custom-call(s32[3]{0:T(128)S(1)} %pad_add_fusion.info_ref, bf16[1024,128]{1,0:T(8,128)(2,1)S(1)} %shard_map.56.refs_0_, bf16[1024,128]{1,0:T(8,128)(2,1)S(1)} %shard_map.59.refs_1_, bf16[1024,128]{1,0:T(8,128)(2,1)S(1)} %shard_map.62.refs_2_, ...), custom_call_target="tpu_custom_call" | custom-call | tf_op jit(solution)/shard_map/pallas_call | solution.py:29
  200.3 5.9 %collective-permute-done.31.refs_3_ = bf16[512,256]{1,0:T(8,128)(2,1)S(1)} collective-permute-done((bf16[512,256]{1,0:T(8,128)(2,1)S(1)}, bf16[512,256]{1,0:T(8,128)(2,1)S(1)}, u32[]{:S(2)}, u32[]{:S(2)}) %collective-permute-start.31) | collective-permute-done | bytes 262176 | tf_op jit(solution)/shard_map/ppermute | solution.py:453
  206.2 1.6 shard_map.77
  (78 shorter events, 39.4 us)
Async XLA Ops:
  3.2 19.0 %collective-permute-start.1 = (bf16[512,640]{1,0:T(8,128)(2,1)}, bf16[512,640]{1,0:T(8,128)(2,1)}, u32[]{:S(2)}, u32[]{:S(2)}) collective-permute-start(bf16[512,640]{1,0:T(8,128)(2,1)} %get-tuple-element.59), channel_id=1, source_target_pairs={{0,4},{4,0},{8,12},{12,8},{16,20},{20,16},{24,28},{28,24},{1,5},{5... | collective-permute-start | bytes 1966088 | tf_op jit(solution)/shard_map/ppermute | solution.py:453
  9.4 40.3 %collective-permute-start.2 = (bf16[512,640]{1,0:T(8,128)(2,1)}, bf16[512,640]{1,0:T(8,128)(2,1)}, u32[]{:S(2)}, u32[]{:S(2)}) collective-permute-start(bf16[512,640]{1,0:T(8,128)(2,1)} %get-tuple-element.61), channel_id=1, source_target_pairs={{0,4},{4,0},{8,12},{12,8},{16,20},{20,16},{24,28},{28,24},{1,5},{5... | collective-permute-start | bytes 1966088 | tf_op jit(solution)/shard_map/ppermute | solution.py:453
  13.3 46.7 %collective-permute-start = (bf16[512,640]{1,0:T(8,128)(2,1)}, bf16[512,640]{1,0:T(8,128)(2,1)S(1)}, u32[]{:S(2)}, u32[]{:S(2)}) collective-permute-start(bf16[512,640]{1,0:T(8,128)(2,1)} %get-tuple-element.58), channel_id=1, source_target_pairs={{0,4},{4,0},{8,12},{12,8},{16,20},{20,16},{24,28},{28,24},{1,5},{5... | collective-permute-start | bytes 1966088 | tf_op jit(solution)/shard_map/ppermute | solution.py:453
  15.1 46.1 %collective-permute-start.23 = (bf16[512,640]{1,0:T(8,128)(2,1)}, bf16[512,640]{1,0:T(8,128)(2,1)}, u32[]{:S(2)}, u32[]{:S(2)}) collective-permute-start(bf16[512,640]{1,0:T(8,128)(2,1)} %get-tuple-element.63.k_ref.kc.k_pair), channel_id=1, source_target_pairs={{0,8},{4,12},{8,16},{12,20},{16,24},{20,28},{1,9},{5,13},{9,17},{1... | collective-permute-start | bytes 1966088 | tf_op jit(solution)/shard_map/ppermute | solution.py:453
  19.4 43.1 %collective-permute-start.19 = (bf16[512,640]{1,0:T(8,128)(2,1)}, bf16[512,640]{1,0:T(8,128)(2,1)}, u32[]{:S(2)}, u32[]{:S(2)}) collective-permute-start(bf16[512,640]{1,0:T(8,128)(2,1)} %get-tuple-element.64.v_ref.refs_0_.vc.v_pair), channel_id=1, source_target_pairs={{8,16},{12,20},{16,24},{20,28},{9,17},{13,21},{17,25},{21,29},{10,... | collective-permute-start | bytes 1966088 | tf_op jit(solution)/shard_map/ppermute | solution.py:453
  22.1 27.5 %collective-permute-start.3 = (f32[8,512]{1,0:T(8,128)S(1)}, f32[8,512]{1,0:T(8,128)S(1)}, u32[]{:S(2)}, u32[]{:S(2)}) collective-permute-start(f32[8,512]{1,0:T(8,128)S(1)} %get-tuple-element.62), channel_id=1, source_target_pairs={{0,4},{4,0},{8,12},{12,8},{16,20},{20,16},{24,28},{28,24},{1,5},{5... | collective-permute-start | bytes 49160 | tf_op jit(solution)/shard_map/ppermute | solution.py:453
  54.9 23.0 %collective-permute-start.13 = (bf16[640,256]{1,0:T(8,128)(2,1)S(1)}, bf16[640,256]{1,0:T(8,128)(2,1)S(1)}, u32[]{:S(2)}, u32[]{:S(2)}) collective-permute-start(bf16[640,256]{1,0:T(8,128)(2,1)S(1)} %get-tuple-element.84), channel_id=1, source_target_pairs={{0,8},{4,12},{24,16},{28,20},{1,9},{5,13},{25,17},{29,21},{2,10},{... | collective-permute-start | bytes 983048 | tf_op jit(solution)/shard_map/ppermute | solution.py:453
  58.6 13.7 %collective-permute-start.25 = (bf16[512,256]{1,0:T(8,128)(2,1)S(1)}, bf16[512,256]{1,0:T(8,128)(2,1)S(1)}, u32[]{:S(2)}, u32[]{:S(2)}) collective-permute-start(bf16[512,256]{1,0:T(8,128)(2,1)S(1)} %get-tuple-element.99), channel_id=1, source_target_pairs={{0,8},{4,12},{24,16},{28,20},{1,9},{5,13},{25,17},{29,21},{2,10},{... | collective-permute-start | bytes 786440 | tf_op jit(solution)/shard_map/ppermute | solution.py:453
  59.9 19.4 %collective-permute-start.10 = (bf16[640,256]{1,0:T(8,128)(2,1)S(1)}, bf16[640,256]{1,0:T(8,128)(2,1)S(1)}, u32[]{:S(2)}, u32[]{:S(2)}) collective-permute-start(bf16[640,256]{1,0:T(8,128)(2,1)S(1)} %get-tuple-element.80), channel_id=1, source_target_pairs={{0,8},{4,12},{24,16},{28,20},{1,9},{5,13},{25,17},{29,21},{2,10},{... | collective-permute-start | bytes 983048 | tf_op jit(solution)/shard_map/ppermute | solution.py:453
  61.3 25.1 %collective-permute-start.7 = (bf16[640,256]{1,0:T(8,128)(2,1)S(1)}, bf16[640,256]{1,0:T(8,128)(2,1)S(1)}, u32[]{:S(2)}, u32[]{:S(2)}) collective-permute-start(bf16[640,256]{1,0:T(8,128)(2,1)S(1)} %get-tuple-element.76), channel_id=1, source_target_pairs={{0,8},{4,12},{24,16},{28,20},{1,9},{5,13},{25,17},{29,21},{2,10},{... | collective-permute-start | bytes 983048 | tf_op jit(solution)/shard_map/ppermute | solution.py:453
  62.6 30.8 %collective-permute-start.4 = (bf16[640,256]{1,0:T(8,128)(2,1)S(1)}, bf16[640,256]{1,0:T(8,128)(2,1)S(1)}, u32[]{:S(2)}, u32[]{:S(2)}) collective-permute-start(bf16[640,256]{1,0:T(8,128)(2,1)S(1)} %get-tuple-element.72), channel_id=1, source_target_pairs={{0,8},{4,12},{24,16},{28,20},{1,9},{5,13},{25,17},{29,21},{2,10},{... | collective-permute-start | bytes 983048 | tf_op jit(solution)/shard_map/ppermute | solution.py:453
  72.3 29.5 %collective-permute-start.16 = (bf16[512,384]{1,0:T(8,128)(2,1)S(1)}, bf16[512,384]{1,0:T(8,128)(2,1)S(1)}, u32[]{:S(2)}, u32[]{:S(2)}) collective-permute-start(bf16[512,384]{1,0:T(8,128)(2,1)S(1)} %get-tuple-element.88), channel_id=1, source_target_pairs={{0,8},{4,12},{24,16},{28,20},{1,9},{5,13},{25,17},{29,21},{2,10},{... | collective-permute-start | bytes 1179656 | tf_op jit(solution)/shard_map/ppermute | solution.py:453
  77.9 24.7 %collective-permute-start.22 = (bf16[1,512,384]{2,1,0:T(8,128)(2,1)S(1)}, bf16[1,512,384]{2,1,0:T(8,128)(2,1)S(1)}, u32[]{:S(2)}, u32[]{:S(2)}) collective-permute-start(bf16[1,512,384]{2,1,0:T(8,128)(2,1)S(1)} %get-tuple-element.92), channel_id=1, source_target_pairs={{8,16},{12,20},{9,17},{13,21},{10,18},{14,22},{11,19},{15,23}} | collective-permute-start | bytes 1179656 | tf_op jit(solution)/shard_map/ppermute | solution.py:453
  79.3 24.7 %collective-permute-start.14 = (bf16[640,256]{1,0:T(8,128)(2,1)S(1)}, bf16[640,256]{1,0:T(8,128)(2,1)S(1)}, u32[]{:S(2)}, u32[]{:S(2)}) collective-permute-start(bf16[640,256]{1,0:T(8,128)(2,1)S(1)} %get-tuple-element.86), channel_id=1, source_target_pairs={{8,16},{12,20},{16,8},{20,12},{9,17},{13,21},{17,9},{21,13},{10,18... | collective-permute-start | bytes 983048 | tf_op jit(solution)/shard_map/ppermute | solution.py:453
  86.3 16.9 %collective-permute-start.26 = (bf16[512,256]{1,0:T(8,128)(2,1)S(1)}, bf16[512,256]{1,0:T(8,128)(2,1)S(1)}, u32[]{:S(2)}, u32[]{:S(2)}) collective-permute-start(bf16[512,256]{1,0:T(8,128)(2,1)S(1)} %get-tuple-element.101), channel_id=1, source_target_pairs={{8,16},{12,20},{16,8},{20,12},{9,17},{13,21},{17,9},{21,13},{10,18... | collective-permute-start | bytes 786440 | tf_op jit(solution)/shard_map/ppermute | solution.py:453
  93.4 40.6 %collective-permute-start.24 = (bf16[512,640]{1,0:T(8,128)(2,1)}, bf16[512,640]{1,0:T(8,128)(2,1)S(1)}, u32[]{:S(2)}, u32[]{:S(2)}) collective-permute-start(bf16[512,640]{1,0:T(8,128)(2,1)} %collective-permute-done.1.k_ref.k_pair.kc), channel_id=1, source_target_pairs={{0,8},{4,12},{8,16},{12,20},{16,24},{20,28},{1,9},{5,13},{9,17},{1... | collective-permute-start | bytes 1966088 | tf_op jit(solution)/shard_map/ppermute | solution.py:453
  101.8 3.1 %collective-permute-start.11 = (bf16[640,256]{1,0:T(8,128)(2,1)S(1)}, bf16[640,256]{1,0:T(8,128)(2,1)S(1)}, u32[]{:S(2)}, u32[]{:S(2)}) collective-permute-start(bf16[640,256]{1,0:T(8,128)(2,1)S(1)} %get-tuple-element.82), channel_id=1, source_target_pairs={{8,16},{12,20},{16,8},{20,12},{9,17},{13,21},{17,9},{21,13},{10,18... | collective-permute-start | bytes 983048 | tf_op jit(solution)/shard_map/ppermute | solution.py:453
  102.6 33.6 %collective-permute-start.21 = (bf16[512,640]{1,0:T(8,128)(2,1)}, bf16[512,640]{1,0:T(8,128)(2,1)S(1)}, u32[]{:S(2)}, u32[]{:S(2)}) collective-permute-start(bf16[512,640]{1,0:T(8,128)(2,1)} %collective-permute-done.2.v_ref.refs_1_.refs_0_.v_pair.vc), channel_id=1, source_target_pairs={{16,24},{20,28},{17,25},{21,29},{18,26},{22,30},{19,27},{23,31}} | collective-permute-start | bytes 1966088 | tf_op jit(solution)/shard_map/ppermute | solution.py:453
  103.3 3.7 %collective-permute-start.8 = (bf16[640,256]{1,0:T(8,128)(2,1)S(1)}, bf16[640,256]{1,0:T(8,128)(2,1)S(1)}, u32[]{:S(2)}, u32[]{:S(2)}) collective-permute-start(bf16[640,256]{1,0:T(8,128)(2,1)S(1)} %get-tuple-element.78), channel_id=1, source_target_pairs={{8,16},{12,20},{16,8},{20,12},{9,17},{13,21},{17,9},{21,13},{10,18... | collective-permute-start | bytes 983048 | tf_op jit(solution)/shard_map/ppermute | solution.py:453
  104.0 28.6 %collective-permute-start.5 = (bf16[640,256]{1,0:T(8,128)(2,1)S(1)}, bf16[640,256]{1,0:T(8,128)(2,1)S(1)}, u32[]{:S(2)}, u32[]{:S(2)}) collective-permute-start(bf16[640,256]{1,0:T(8,128)(2,1)S(1)} %get-tuple-element.74), channel_id=1, source_target_pairs={{8,16},{12,20},{16,8},{20,12},{9,17},{13,21},{17,9},{21,13},{10,18... | collective-permute-start | bytes 983048 | tf_op jit(solution)/shard_map/ppermute | solution.py:453
  104.8 33.5 %collective-permute-start.17 = (bf16[512,384]{1,0:T(8,128)(2,1)S(1)}, bf16[512,384]{1,0:T(8,128)(2,1)S(1)}, u32[]{:S(2)}, u32[]{:S(2)}) collective-permute-start(bf16[512,384]{1,0:T(8,128)(2,1)S(1)} %get-tuple-element.90), channel_id=1, source_target_pairs={{8,16},{12,20},{16,8},{20,12},{9,17},{13,21},{17,9},{21,13},{10,18... | collective-permute-start | bytes 1179656 | tf_op jit(solution)/shard_map/ppermute | solution.py:453
  106.9 79.8 %collective-permute-start.20 = (bf16[2,512,384]{2,1,0:T(8,128)(2,1)S(1)}, bf16[2,512,384]{2,1,0:T(8,128)(2,1)S(1)}, u32[]{:S(2)}, u32[]{:S(2)}) collective-permute-start(bf16[2,512,384]{2,1,0:T(8,128)(2,1)S(1)} %get-tuple-element.91), channel_id=1, source_target_pairs={{0,8},{4,12},{1,9},{5,13},{2,10},{6,14},{3,11},{7,15}} | collective-permute-start | bytes 2359304 | tf_op jit(solution)/shard_map/ppermute | solution.py:453
  132.7 13.2 %collective-permute-start.15 = (bf16[640,256]{1,0:T(8,128)(2,1)S(1)}, bf16[640,256]{1,0:T(8,128)(2,1)S(1)}, u32[]{:S(2)}, u32[]{:S(2)}) collective-permute-start(bf16[640,256]{1,0:T(8,128)(2,1)S(1)} %shard_map.64.made_ref), channel_id=1, source_target_pairs={{8,0},{12,4},{16,24},{20,28},{9,1},{13,5},{17,25},{21,29},{10,2},{... | collective-permute-start | bytes 983048 | tf_op jit(solution)/shard_map/ppermute | solution.py:453
  134.0 18.9 %collective-permute-start.12 = (bf16[640,256]{1,0:T(8,128)(2,1)S(1)}, bf16[640,256]{1,0:T(8,128)(2,1)S(1)}, u32[]{:S(2)}, u32[]{:S(2)}) collective-permute-start(bf16[640,256]{1,0:T(8,128)(2,1)S(1)} %shard_map.61.made_ref), channel_id=1, source_target_pairs={{8,0},{12,4},{16,24},{20,28},{9,1},{13,5},{17,25},{21,29},{10,2},{... | collective-permute-start | bytes 983048 | tf_op jit(solution)/shard_map/ppermute | solution.py:453
  136.2 23.7 %collective-permute-start.9 = (bf16[640,256]{1,0:T(8,128)(2,1)S(1)}, bf16[640,256]{1,0:T(8,128)(2,1)S(1)}, u32[]{:S(2)}, u32[]{:S(2)}) collective-permute-start(bf16[640,256]{1,0:T(8,128)(2,1)S(1)} %shard_map.58.made_ref), channel_id=1, source_target_pairs={{8,0},{12,4},{16,24},{20,28},{9,1},{13,5},{17,25},{21,29},{10,2},{... | collective-permute-start | bytes 983048 | tf_op jit(solution)/shard_map/ppermute | solution.py:453
  138.3 28.6 %collective-permute-start.6 = (bf16[640,256]{1,0:T(8,128)(2,1)S(1)}, bf16[640,256]{1,0:T(8,128)(2,1)S(1)}, u32[]{:S(2)}, u32[]{:S(2)}) collective-permute-start(bf16[640,256]{1,0:T(8,128)(2,1)S(1)} %shard_map.55.made_ref), channel_id=1, source_target_pairs={{8,0},{12,4},{16,24},{20,28},{9,1},{13,5},{17,25},{21,29},{10,2},{... | collective-permute-start | bytes 983048 | tf_op jit(solution)/shard_map/ppermute | solution.py:453
  145.9 40.9 %collective-permute-start.18 = (bf16[512,384]{1,0:T(8,128)(2,1)S(1)}, bf16[512,384]{1,0:T(8,128)(2,1)S(1)}, u32[]{:S(2)}, u32[]{:S(2)}) collective-permute-start(bf16[512,384]{1,0:T(8,128)(2,1)S(1)} %shard_map.67.refs_4_), channel_id=1, source_target_pairs={{8,0},{12,4},{16,24},{20,28},{9,1},{13,5},{17,25},{21,29},{10,2},{... | collective-permute-start | bytes 1179656 | tf_op jit(solution)/shard_map/ppermute | solution.py:453
  152.9 43.7 %collective-permute-start.28 = (bf16[2,512,256]{2,1,0:T(8,128)(2,1)S(1)}, bf16[2,512,256]{2,1,0:T(8,128)(2,1)S(1)}, u32[]{:S(2)}, u32[]{:S(2)}) collective-permute-start(bf16[2,512,256]{2,1,0:T(8,128)(2,1)S(1)} %get-tuple-element.102), channel_id=1, source_target_pairs={{0,8},{4,12},{1,9},{5,13},{2,10},{6,14},{3,11},{7,15}} | collective-permute-start | bytes 1572872 | tf_op jit(solution)/shard_map/ppermute | solution.py:453
  159.9 36.7 %collective-permute-start.29 = (bf16[1,512,256]{2,1,0:T(8,128)(2,1)S(1)}, bf16[1,512,256]{2,1,0:T(8,128)(2,1)S(1)}, u32[]{:S(2)}, u32[]{:S(2)}) collective-permute-start(bf16[1,512,256]{2,1,0:T(8,128)(2,1)S(1)} %get-tuple-element.103), channel_id=1, source_target_pairs={{8,16},{12,20},{9,17},{13,21},{10,18},{14,22},{11,19},{15,23}} | collective-permute-start | bytes 786440 | tf_op jit(solution)/shard_map/ppermute | solution.py:453
  166.9 29.7 %collective-permute-start.27 = (bf16[512,256]{1,0:T(8,128)(2,1)S(1)}, bf16[512,256]{1,0:T(8,128)(2,1)S(1)}, u32[]{:S(2)}, u32[]{:S(2)}) collective-permute-start(bf16[512,256]{1,0:T(8,128)(2,1)S(1)} %shard_map.74.refs_4_), channel_id=1, source_target_pairs={{8,0},{12,4},{16,24},{20,28},{9,1},{13,5},{17,25},{21,29},{10,2},{... | collective-permute-start | bytes 786440 | tf_op jit(solution)/shard_map/ppermute | solution.py:453
  190.6 15.7 %collective-permute-start.30 = (bf16[512,384]{1,0:T(8,128)(2,1)S(1)}, bf16[512,384]{1,0:T(8,128)(2,1)S(1)}, u32[]{:S(2)}, u32[]{:S(2)}) collective-permute-start(bf16[512,384]{1,0:T(8,128)(2,1)S(1)} %get-tuple-element.107), channel_id=1, source_target_pairs={{0,4},{4,0},{8,12},{12,8},{16,20},{20,16},{24,28},{28,24},{1,5},{5... | collective-permute-start | bytes 1179656 | tf_op jit(solution)/shard_map/ppermute | solution.py:453
  199.8 6.4 %collective-permute-start.31 = (bf16[512,256]{1,0:T(8,128)(2,1)S(1)}, bf16[512,256]{1,0:T(8,128)(2,1)S(1)}, u32[]{:S(2)}, u32[]{:S(2)}) collective-permute-start(bf16[512,256]{1,0:T(8,128)(2,1)S(1)} %get-tuple-element.108), channel_id=1, source_target_pairs={{0,4},{4,0},{8,12},{12,8},{16,20},{20,16},{24,28},{28,24},{1,5},{5... | collective-permute-start | bytes 786440 | tf_op jit(solution)/shard_map/ppermute | solution.py:453
  (6 other events, 79.4 us)

commit v2 on v1

--- a/solution.py
+++ b/solution.py
@@ -71,16 +71,19 @@
     )
 
 
-def stack_columns(arrays, cuts):
-    count = len(arrays)
-
-    def body(*refs):
-        for (lo, hi), out in zip(cuts, refs[count:]):
-            for at, ref in enumerate(refs[:count]):
-                out[at] = ref[:, lo:hi]
-
-    shapes = [(count, arrays[0].shape[0], hi - lo) for lo, hi in cuts]
-    return call(body, [VM] * count, [sds(shape, BF16) for shape in shapes], arrays)
+def late_columns(first, second, cuts):
+    count = len(cuts)
+
+    def body(a_ref, b_ref, *outs):
+        for (lo, hi), stack, single in zip(cuts, outs, outs[count:]):
+            stack[0] = a_ref[:, lo:hi]
+            stack[1] = b_ref[:, lo:hi]
+            single[...] = b_ref[:, lo:hi]
+
+    rows = first.shape[0]
+    shapes = [(2, rows, hi - lo) for lo, hi in cuts] + [(rows, hi - lo) for lo, hi in cuts]
+    outs = call(body, [VM] * 2, [sds(shape, BF16) for shape in shapes], (first, second))
+    return outs[:count], outs[count:]
 
 
 def gate_parts(keys, w_in, hidden_dim):
@@ -164,60 +167,79 @@
     count = len(in_cuts) + len(out_cuts)
 
     def body(info_ref, k_ref, s_ref, wout_ref, h_ref, t_ref, a_ref, gin_ref, gout_ref, *o):
+        sends = [o[i] for i in range(count - 2)]
+        sends += [o[count - 2].at[:width, :], o[count - 2].at[width:, :]]
+        keeps = o[count - 1 :]
         pre_gate, pre_up = back_parts(s_ref[...], wout_ref[info_ref[0]], t_ref[...], a_ref[...])
         for at, (lo, hi) in enumerate(in_cuts):
             size = hi - lo
             for start, base, pre in ((0, lo, pre_gate), (size, hidden_dim + lo, pre_up)):
                 part = gin_ref[:, base : base + size]
                 part += dot(k_ref[...], pre[:, lo:hi], ((0,), (0,)))
-                o[at][:, start : start + size] = part.astype(BF16)
-                o[count + at][:, start : start + size] = part
+                sends[at][:, start : start + size] = part.astype(BF16)
+                keeps[at][:, start : start + size] = part
         for at, (lo, hi) in enumerate(out_cuts, len(in_cuts)):
             part = gout_ref[:, lo:hi] + dot(h_ref[...], s_ref[:, lo:hi], ((0,), (0,)))
-            o[at][...] = part.astype(BF16)
-            o[count + at][...] = part
+            sends[at][...] = part.astype(BF16)
+            keeps[at][...] = part
 
     shapes = [(width, 2 * (hi - lo)) for lo, hi in in_cuts]
     shapes += [(hidden_dim, hi - lo) for lo, hi in out_cuts]
+    joined = (shapes[-2][0] + shapes[-1][0], shapes[-1][1])
     outs = call(
         body,
         [SM] + [VM] * 8,
-        [sds(s, BF16) for s in shapes] + [sds(s, F32) for s in shapes],
+        [sds(s, BF16) for s in shapes[:-2] + [joined]] + [sds(s, F32) for s in shapes],
         (info, keys, scaled, fast_out, *gates, gin, gout),
     )
-    return outs[:count], outs[count:]
-
-
-def add_chunk(kept, got):
+    return outs[: count - 1], outs[count - 1 :]
+
+
+def add_chunk(kept, got, first):
+    rows = kept.shape[0]
+
     def body(kept_ref, got_ref, send_ref, sum_ref):
-        total = kept_ref[...] + got_ref[...].astype(F32)
+        total = kept_ref[...] + got_ref[first : first + rows, :].astype(F32)
         send_ref[...] = total.astype(BF16)
         sum_ref[...] = total
 
     return call(body, [VM] * 2, [sds(kept.shape, BF16), sds(kept.shape, F32)], (kept, got))
 
 
-def new_weights(info, mine, others, fast, lo, hi, factor, paired):
+def column_norms(info, fast_in, fast_out):
+    def body(info_ref, win_ref, wout_ref, in_ref, out_ref):
+        for ref, out in ((win_ref, in_ref), (wout_ref, out_ref)):
+            old = ref[info_ref[0]].astype(F32)
+            out[...] = jnp.sqrt(jnp.sum(old * old, axis=0, keepdims=True))
+
+    return call(
+        body,
+        [SM, VM, VM],
+        [sds((1, fast_in.shape[2]), F32), sds((1, fast_out.shape[2]), F32)],
+        (info, fast_in, fast_out),
+    )
+
+
+def new_weights(info, mine, others, fast, norms, lo, hi, factor, paired):
     count = len(others)
     size = hi - lo
     half = fast.shape[2] // 2
 
     def body(info_ref, a_ref, *rest):
-        w_ref, o_ref = rest[count:]
+        w_ref, norm_ref, o_ref = rest[count:]
         keep = info_ref[0]
         spans = [(0, lo)] + ([(size, half + lo)] if paired else [])
         for start, col in spans:
             total = a_ref[:, start : start + size]
             for b_ref in rest[:count]:
                 total += b_ref[:, start : start + size].astype(F32)
-            old = w_ref[keep, :, col : col + size].astype(F32)
-            moved = old + total * factor
-            old_norm = jnp.sqrt(jnp.sum(old * old, axis=0, keepdims=True))
+            moved = w_ref[keep, :, col : col + size].astype(F32) + total * factor
             new_norm = jnp.sqrt(jnp.sum(moved * moved, axis=0, keepdims=True))
-            o_ref[:, start : start + size] = (moved * (old_norm / (new_norm + EPS))).astype(BF16)
-
-    return call(
-        body, [SM] + [VM] * (count + 2), [sds(mine.shape, BF16)], (info, mine, *others, fast)
+            ratio = norm_ref[:, col : col + size] / (new_norm + EPS)
+            o_ref[:, start : start + size] = (moved * ratio).astype(BF16)
+
+    return call(
+        body, [SM] + [VM] * (count + 3), [sds(mine.shape, BF16)], (info, mine, *others, fast, norms)
     )[0]
 
 
@@ -247,53 +269,48 @@
     )[0]
 
 
-def apply_chunk(info, hiddens, made, got, parts, late, lo, hi):
+def apply_chunk(info, side, hiddens, made, got, left, late, lo, hi):
     rows = hiddens[0].shape[0] // 2
     size = hi - lo
     count = len(hiddens)
-    (own_sum, own_at, own_p), (oth_sum, oth_at, oth_p) = parts
+    sums, base, weights = left
     vals = [array for group in late for array, _, _ in group]
 
     def body(info_ref, *refs):
         hid = refs[:count]
         made_ref, got_ref = refs[count : count + 2]
         val_refs = list(refs[count + 2 : count + 2 + len(vals)])
-        att = refs[count + 2 + len(vals) : -2]
-        own_ref, oth_ref = refs[-2:]
+        sum_ref, p_ref, out = refs[-3:]
         groups = [[(val_refs.pop(0), *place) for _, *place in group] for group in late]
 
         def values(group, head):
             total = None
-            for ref, base, layer_at in group:
-                col = lo - base + head * ADIM
+            for ref, first, layer_at in group:
+                col = lo - first + head * ADIM
                 cols = slice(col, col + ADIM)
                 piece = ref[:, cols] if layer_at is None else ref[layer_at, :, cols]
                 total = piece if total is None else total + piece
             return total
 
         def run(w_ref):
-            for start, out, sum_ref, base, p_ref, order in (
-                (rows, oth_ref, att[2], oth_at, att[3], (1, 0)),
-                (0, own_ref, att[0], own_at, att[1], (0, 1)),
-            ):
-                total = sum_ref[:, base : base + size]
-                row = 0
-                for ref in hid:
-                    part = ref.shape[1]
-                    total += dot(
-                        ref[start : start + rows, :], w_ref[row : row + part, :], ((1,), (0,))
-                    )
-                    row += part
-                for head in range(size // ADIM):
-                    col = head * ADIM
-                    mixed = total[:, col : col + ADIM]
-                    for place, which in enumerate(order):
-                        p = p_ref[base // ADIM + head, :, place * rows : (place + 1) * rows]
-                        v = values(groups[which], head)
-                        if place == 1:
-                            v = jnp.where(info_ref[0] == which, jnp.zeros_like(v), v)
-                        mixed += dot(p, v, ((1,), (0,)))
-                    out[:, col : col + ADIM] = mixed.astype(BF16)
+            total = sum_ref[:, base : base + size]
+            row = 0
+            for ref in hid:
+                part = ref.shape[1]
+                total += dot(
+                    ref[side * rows : (side + 1) * rows, :], w_ref[row : row + part, :], ((1,), (0,))
+                )
+                row += part
+            for head in range(size // ADIM):
+                col = head * ADIM
+                mixed = total[:, col : col + ADIM]
+                for place, which in enumerate((side, 1 - side)):
+                    p = p_ref[base // ADIM + head, :, place * rows : (place + 1) * rows]
+                    v = values(groups[which], head)
+                    if place == 1:
+                        v = jnp.where(info_ref[0] == which, jnp.zeros_like(v), v)
+                    mixed += dot(p, v, ((1,), (0,)))
+                out[:, col : col + ADIM] = mixed.astype(BF16)
 
         @pl.when(info_ref[2] == 1)
         def _():
@@ -305,10 +322,10 @@
 
     return call(
         body,
-        [SM] + [VM] * (count + 2 + len(vals) + 4),
-        [sds((rows, size), BF16)] * 2,
-        (info, *hiddens, made, got, *vals, own_sum, own_p, oth_sum, oth_p),
-    )
+        [SM] + [VM] * (count + 2 + len(vals) + 2),
+        [sds((rows, size), BF16)],
+        (info, *hiddens, made, got, *vals, sums, weights),
+    )[0]
 
 
 def attention(info, side, heads, q, k_own, v_own, k_oth, v_oth, pk_own, pk_oth):
@@ -459,8 +476,9 @@
     out_cuts = [(0, middle), (middle, head_width)]
 
     qkv = pltpu.with_memory_space_constraint(qkv, pltpu.HBM)
-    k_away, k_own = cut_blocks(info, qkv, [(1, False), (1, True)], head_width)
+    (k_away,) = cut_blocks(info, qkv, [(1, False)], head_width)
     k_oth = permute(k_away, swap_pairs)
+    (k_own,) = cut_blocks(info, qkv, [(1, True)], head_width)
     pk_own = permute(k_own, next_pairs)
     v_away, v_own = cut_blocks(info, qkv, [(2, False), (2, True)], head_width)
     rate_own, rate_send = rate_rows(info, step_size)
@@ -472,15 +490,14 @@
     if line == 4:
         own_early = permute(v_own, along([(1, 2), (2, 3)]))
         oth_early = permute(v_oth, along([(2, 3)]))
-        stacks = stack_columns((v_own, v_oth), out_cuts)
-        singles = stack_columns((v_oth,), out_cuts)
+        stacks, singles = late_columns(v_own, v_oth, out_cuts)
         late_vals = []
         for i, (lo, hi) in enumerate(out_cuts):
             first = permute(stacks[i], along([(0, 1)]))
             second = permute(singles[i], along([(1, 2)]))
             late_vals.append((
                 [(own_early, 0, None), (first, lo, 0)],
-                [(oth_early, 0, None), (first, lo, 1), (second, lo, 0)],
+                [(oth_early, 0, None), (first, lo, 1), (second, lo, None)],
             ))
     else:
         late_vals = [(
@@ -494,25 +511,29 @@
         info, k_oth, scaled, fast_out, gates, gin, gout, in_cuts, out_cuts[1:]
     )
     send, kept = [first[0], *send], [first[1], *kept]
-    plan = [(fast_out, *out_cuts[0], False)]
-    plan += [(fast_in, lo, hi, True) for lo, hi in in_cuts]
-    plan += [(fast_out, lo, hi, False) for lo, hi in out_cuts[1:]]
+    in_norms, out_norms = column_norms(info, fast_in, fast_out)
+    plan = [(fast_out, out_norms, *out_cuts[0], False)]
+    plan += [(fast_in, in_norms, lo, hi, True) for lo, hi in in_cuts]
+    plan += [(fast_out, out_norms, lo, hi, False) for lo, hi in out_cuts[1:]]
 
     made, got = [], []
     if line == 4:
         inward = along([(0, 1), (3, 2)])
         centre = along([(1, 2), (2, 1)])
         outward = along([(1, 0), (2, 3)])
-        for at, (fast, lo, hi, paired) in enumerate(plan):
-            half_sum, total = add_chunk(kept[at], permute(send[at], inward))
+        arrived = [permute(array, inward) for array in send]
+        for at, (fast, norms, lo, hi, paired) in enumerate(plan):
+            first = kept[at - 1].shape[0] if at == len(send) else 0
+            source = arrived[min(at, len(send) - 1)]
+            half_sum, total = add_chunk(kept[at], source, first)
             crossed = [permute(half_sum, centre)]
-            made.append(new_weights(info, total, crossed, fast, lo, hi, factor, paired))
+            made.append(new_weights(info, total, crossed, fast, norms, lo, hi, factor, paired))
             got.append(permute(made[at], outward))
     else:
-        for at, (fast, lo, hi, paired) in enumerate(plan):
+        for at, (fast, norms, lo, hi, paired) in enumerate(plan):
             slots = jnp.where(jnp.arange(2)[:, None, None] == keep, kept[at][None], 0.0)
             total = lax.dynamic_index_in_dim(lax.psum(slots, "ctx"), keep, 0, keepdims=False)
-            made.append(new_weights(info, total, (), fast, lo, hi, factor, paired))
+            made.append(new_weights(info, total, (), fast, norms, lo, hi, factor, paired))
         got = made
 
     heads = head_width // ADIM
@@ -525,12 +546,15 @@
     own_parts, oth_parts = [], []
     for i, (lo, hi) in enumerate(out_cuts):
         at = parts + i if i else 0
-        left = (own_sum, lo, own_p), (
-            (oth_some[0], lo, oth_some[1]) if lo < middle else (oth_rest[0], lo - middle, oth_rest[1])
-        )
-        mine, theirs = apply_chunk(info, hiddens, made[at], got[at], left, late_vals[i], lo, hi)
-        own_parts.append(mine)
+        some = (hiddens, made[at], got[at])
+        if lo < middle:
+            left = (oth_some[0], lo, oth_some[1])
+        else:
+            left = (oth_rest[0], lo - middle, oth_rest[1])
+        theirs = apply_chunk(info, 1, *some, left, late_vals[i], lo, hi)
         oth_parts.append(permute(theirs, swap_pairs))
+        left = (own_sum, lo, own_p)
+        own_parts.append(apply_chunk(info, 0, *some, left, late_vals[i], lo, hi))
     return assemble(info, own_parts, oth_parts, out_cuts)
 
 

time: 210 us -> 199 us (0.948)
  waiting for transfers between devices: 72 us -> 63 us
  starting transfers between devices: 72.3 us -> 67.5 us
  Pallas kernels: 60.6 us -> 64.5 us
    ppermute x32 -> x31, waiting for transfers between devices: 72 us -> 63 us  [permute(): return lax.ppermute(array, 'ctx', pairs)]
    ppermute x32 -> x31, starting transfers between devices: 72.3 us -> 67.5 us  [permute(): return lax.ppermute(array, 'ctx', pairs)]
    pallas_call x32 -> x35, Pallas kernels: 60.6 us -> 64.5 us  [call(): pl.pallas_call(body, in_specs=ins, out_specs=out_specs if out_specs is no...]
  transfers between devices with their start and end apart: 32 -> 31, of which waited for: 12 -> 9; matrix products, arithmetic and copies ran while one was open for 0% -> 0% of each run, Pallas kernels for 27% -> 30%
where the time goes in v2:
time: 199 us; the launch traced here: 198 us
  starting transfers between devices  67.5 us (34%)
  Pallas kernels  64.5 us (32%)
  waiting for transfers between devices  63 us (32%)
  local copies, waits for them, and re-layouts  2.33 us (1%)
    ppermute x31, starting transfers between devices, permute(): return lax.ppermute(array, 'ctx', pairs)  67.5 us
    pallas_call x35, Pallas kernels, call(): pl.pallas_call(body, in_specs=ins, out_specs=out_specs if out_specs is no...  64.5 us
    ppermute x31, waiting for transfers between devices, permute(): return lax.ppermute(array, 'ctx', pairs)  63 us
  transfers between devices with their start and end apart: 31, of which 9 were waited for; matrix products, arithmetic and copies ran while one was open for 0% of the time, Pallas kernels for 30%

profile of v2, /device:TPU:0, one launch (start us, length us, event | category | flops | bytes accessed | tf_op | source)
XLA Modules:
  0.0 198.2 jit_solution(1450432331287375808)
XLA Ops:
  0.1 2.6 %shard_map.47 = bf16[512,640]{1,0:T(8,128)(2,1)} custom-call(s32[3]{0:T(128)S(1)} %pad_add_fusion.info_ref, bf16[3,512,1280]{2,1,0:T(8,128)(2,1)} %qkv_ref.7), custom_call_target="tpu_custom_call" | custom-call | tf_op jit(solution)/shard_map/pallas_call | solution.py:29
  2.7 3.1 %collective-permute-start.1 = (bf16[512,640]{1,0:T(8,128)(2,1)}, bf16[512,640]{1,0:T(8,128)(2,1)}, u32[]{:S(2)}, u32[]{:S(2)}) collective-permute-start(bf16[512,640]{1,0:T(8,128)(2,1)} %shard_map.47), channel_id=1, source_target_pairs={{0,4},{4,0},{8,12},{12,8},{16,20},{20,16},{24,28},{28,24},{1,5},{5... | collective-permute-start | bytes 1966088 | tf_op jit(solution)/shard_map/ppermute | solution.py:470
  5.7 3.1 %shard_map.49 = (bf16[512,640]{1,0:T(8,128)(2,1)}, bf16[512,640]{1,0:T(8,128)(2,1)}) custom-call(s32[3]{0:T(128)S(1)} %pad_add_fusion.info_ref, bf16[3,512,1280]{2,1,0:T(8,128)(2,1)} %qkv_ref.7), custom_call_target="tpu_custom_call" | custom-call | tf_op jit(solution)/shard_map/pallas_call | solution.py:29
  8.9 2.8 %shard_map.46 = (bf16[512,640]{1,0:T(8,128)(2,1)}, bf16[512,640]{1,0:T(8,128)(2,1)S(1)}) custom-call(s32[3]{0:T(128)S(1)} %pad_add_fusion.info_ref, bf16[3,512,1280]{2,1,0:T(8,128)(2,1)} %qkv_ref.7), custom_call_target="tpu_custom_call" | custom-call | tf_op jit(solution)/shard_map/pallas_call | solution.py:29
  12.6 2.0 %collective-permute-start = (bf16[512,640]{1,0:T(8,128)(2,1)}, bf16[512,640]{1,0:T(8,128)(2,1)S(1)}, u32[]{:S(2)}, u32[]{:S(2)}) collective-permute-start(bf16[512,640]{1,0:T(8,128)(2,1)} %get-tuple-element.53), channel_id=1, source_target_pairs={{0,4},{4,0},{8,12},{12,8},{16,20},{20,16},{24,28},{28,24},{1,5},{5... | collective-permute-start | bytes 1966088 | tf_op jit(solution)/shard_map/ppermute | solution.py:470
  14.6 2.6 %shard_map.51.k_ref.kc.k_pair = bf16[512,640]{1,0:T(8,128)(2,1)} custom-call(s32[3]{0:T(128)S(1)} %pad_add_fusion.info_ref, bf16[3,512,1280]{2,1,0:T(8,128)(2,1)} %qkv_ref.7), custom_call_target="tpu_custom_call" | custom-call | tf_op jit(solution)/shard_map/pallas_call | solution.py:29
  17.2 4.3 %collective-permute-start.23 = (bf16[512,640]{1,0:T(8,128)(2,1)}, bf16[512,640]{1,0:T(8,128)(2,1)}, u32[]{:S(2)}, u32[]{:S(2)}) collective-permute-start(bf16[512,640]{1,0:T(8,128)(2,1)} %shard_map.51.k_ref.kc.k_pair), channel_id=1, source_target_pairs={{0,8},{4,12},{8,16},{12,20},{16,24},{20,28},{1,9},{5,13},{9,17},{1... | collective-permute-start | bytes 1966088 | tf_op jit(solution)/shard_map/ppermute | solution.py:470
  21.5 1.5 collective-permute-start.19
  25.7 4.0 %shard_map.52 = (f32[640,1024]{1,0:T(8,128)S(1)}, f32[512,640]{1,0:T(8,128)S(1)}) custom-call(s32[3]{0:T(128)S(1)} %pad_add_fusion.info_ref, bf16[512,640]{1,0:T(8,128)(2,1)} %shard_map.51.k_ref.kc.k_pair, bf16[512,640]{1,0:T(8,128)(2,1)} %get-tuple-element.57.v_ref.a_ref.vc.v_pair, f32[8,512]{1,0:T(8,128)S(1)} %get-tuple-element.58.rate_ref, ...), custom_call_target="tpu_custom_call" | custom-call | tf_op jit(solution)/shard_map/pallas_call | solution.py:29
  29.7 2.3 %shard_map.48 = (bf16[512,512]{1,0:T(8,128)(2,1)S(1)}, f32[512,512]{1,0:T(8,128)S(1)}, f32[512,512]{1,0:T(8,128)S(1)}) custom-call(s32[3]{0:T(128)S(1)} %pad_add_fusion.info_ref, bf16[512,640]{1,0:T(8,128)(2,1)} %collective-permute-done.1.k_ref.k_pair.kc, bf16[2,640,1024]{2,1,0:T(8,128)(2,1)S(1)} %copy-done), custom_call_target="tpu_custom_call" | custom-call | tf_op jit(solution)/shard_map/pallas_call | solution.py:29
  32.0 17.1 %collective-permute-done.3.rate_ref = f32[8,512]{1,0:T(8,128)S(1)} collective-permute-done((f32[8,512]{1,0:T(8,128)S(1)}, f32[8,512]{1,0:T(8,128)S(1)}, u32[]{:S(2)}, u32[]{:S(2)}) %collective-permute-start.3) | collective-permute-done | bytes 16416 | tf_op jit(solution)/shard_map/ppermute | solution.py:470
  49.1 1.8 shard_map.53
  51.0 3.4 %shard_map.54 = (bf16[640,256]{1,0:T(8,128)(2,1)S(1)}, bf16[640,256]{1,0:T(8,128)(2,1)S(1)}, bf16[640,256]{1,0:T(8,128)(2,1)S(1)}, bf16[1152,256]{1,0:T(8,128)(2...) custom-call(s32[3]{0:T(128)S(1)} %pad_add_fusion.info_ref, ...), custom_call_target="tpu_custom_call" | custom-call | tf_op jit(solution)/shard_map/pallas_call | solution.py:29
  54.4 3.7 %collective-permute-start.10 = (bf16[640,256]{1,0:T(8,128)(2,1)S(1)}, bf16[640,256]{1,0:T(8,128)(2,1)S(1)}, u32[]{:S(2)}, u32[]{:S(2)}) collective-permute-start(bf16[640,256]{1,0:T(8,128)(2,1)S(1)} %get-tuple-element.74), channel_id=1, source_target_pairs={{0,8},{4,12},{24,16},{28,20},{1,9},{5,13},{25,17},{29,21},{2,10},{... | collective-permute-start | bytes 983048 | tf_op jit(solution)/shard_map/ppermute | solution.py:470
  66.9 6.3 %collective-permute-done.7.got_ref = bf16[640,256]{1,0:T(8,128)(2,1)S(1)} collective-permute-done((bf16[640,256]{1,0:T(8,128)(2,1)S(1)}, bf16[640,256]{1,0:T(8,128)(2,1)S(1)}, u32[]{:S(2)}, u32[]{:S(2)}) %collective-permute-start.7) | collective-permute-done | bytes 327712 | tf_op jit(solution)/shard_map/ppermute | solution.py:470
  73.9 14.8 %collective-permute-done.4.got_ref = bf16[640,256]{1,0:T(8,128)(2,1)S(1)} collective-permute-done((bf16[640,256]{1,0:T(8,128)(2,1)S(1)}, bf16[640,256]{1,0:T(8,128)(2,1)S(1)}, u32[]{:S(2)}, u32[]{:S(2)}) %collective-permute-start.4) | collective-permute-done | bytes 327712 | tf_op jit(solution)/shard_map/ppermute | solution.py:470
  88.6 4.4 %collective-permute-start.24 = (bf16[512,640]{1,0:T(8,128)(2,1)}, bf16[512,640]{1,0:T(8,128)(2,1)S(1)}, u32[]{:S(2)}, u32[]{:S(2)}) collective-permute-start(bf16[512,640]{1,0:T(8,128)(2,1)} %collective-permute-done.1.k_ref.k_pair.kc), channel_id=1, source_target_pairs={{0,8},{4,12},{8,16},{12,20},{16,24},{20,28},{1,9},{5,13},{9,17},{1... | collective-permute-start | bytes 1966088 | tf_op jit(solution)/shard_map/ppermute | solution.py:470
  94.8 6.5 %collective-permute-done.13.got_ref = bf16[1152,256]{1,0:T(8,128)(2,1)S(1)} collective-permute-done((bf16[1152,256]{1,0:T(8,128)(2,1)S(1)}, bf16[1152,256]{1,0:T(8,128)(2,1)S(1)}, u32[]{:S(2)}, u32[]{:S(2)}) %collective-permute-start.13) | collective-permute-done | bytes 589856 | tf_op jit(solution)/shard_map/ppermute | solution.py:470
  103.4 22.5 %collective-permute-start.20 = (bf16[2,512,384]{2,1,0:T(8,128)(2,1)S(1)}, bf16[2,512,384]{2,1,0:T(8,128)(2,1)S(1)}, u32[]{:S(2)}, u32[]{:S(2)}) collective-permute-start(bf16[2,512,384]{2,1,0:T(8,128)(2,1)S(1)} %get-tuple-element.86), channel_id=1, source_target_pairs={{0,8},{4,12},{1,9},{5,13},{2,10},{6,14},{3,11},{7,15}} | collective-permute-start | bytes 2359304 | tf_op jit(solution)/shard_map/ppermute | solution.py:470
  136.8 4.0 %collective-permute-done.12.got_ref = bf16[640,256]{1,0:T(8,128)(2,1)S(1)} collective-permute-done((bf16[640,256]{1,0:T(8,128)(2,1)S(1)}, bf16[640,256]{1,0:T(8,128)(2,1)S(1)}, u32[]{:S(2)}, u32[]{:S(2)}) %collective-permute-start.12) | collective-permute-done | bytes 327712 | tf_op jit(solution)/shard_map/ppermute | solution.py:470
  140.8 3.9 %collective-permute-start.27 = (bf16[2,512,256]{2,1,0:T(8,128)(2,1)S(1)}, bf16[2,512,256]{2,1,0:T(8,128)(2,1)S(1)}, u32[]{:S(2)}, u32[]{:S(2)}) collective-permute-start(bf16[2,512,256]{2,1,0:T(8,128)(2,1)S(1)} %get-tuple-element.93), channel_id=1, source_target_pairs={{0,8},{4,12},{1,9},{5,13},{2,10},{6,14},{3,11},{7,15}} | collective-permute-start | bytes 1572872 | tf_op jit(solution)/shard_map/ppermute | solution.py:470
  144.7 3.1 %collective-permute-done.9.got_ref = bf16[640,256]{1,0:T(8,128)(2,1)S(1)} collective-permute-done((bf16[640,256]{1,0:T(8,128)(2,1)S(1)}, bf16[640,256]{1,0:T(8,128)(2,1)S(1)}, u32[]{:S(2)}, u32[]{:S(2)}) %collective-permute-start.9) | collective-permute-done | bytes 327712 | tf_op jit(solution)/shard_map/ppermute | solution.py:470
  149.9 5.0 %collective-permute-done.6.got_ref = bf16[640,256]{1,0:T(8,128)(2,1)S(1)} collective-permute-done((bf16[640,256]{1,0:T(8,128)(2,1)S(1)}, bf16[640,256]{1,0:T(8,128)(2,1)S(1)}, u32[]{:S(2)}, u32[]{:S(2)}) %collective-permute-start.6) | collective-permute-done | bytes 327712 | tf_op jit(solution)/shard_map/ppermute | solution.py:470
  155.5 4.9 %collective-permute-done.15.got_ref = bf16[640,256]{1,0:T(8,128)(2,1)S(1)} collective-permute-done((bf16[640,256]{1,0:T(8,128)(2,1)S(1)}, bf16[640,256]{1,0:T(8,128)(2,1)S(1)}, u32[]{:S(2)}, u32[]{:S(2)}) %collective-permute-start.15) | collective-permute-done | bytes 327712 | tf_op jit(solution)/shard_map/ppermute | solution.py:470
  162.0 5.7 %shard_map.76 = (f32[512,384]{1,0:T(8,128)S(1)}, bf16[3,512,1024]{2,1,0:T(8,128)(2,1)S(1)}) custom-call(s32[3]{0:T(128)S(1)} %pad_add_fusion.info_ref, bf16[512,640]{1,0:T(8,128)(2,1)S(1)} %collective-permute-done.qb_ref.q_ref, bf16[512,640]{1,0:T(8,128)(2,1)} %collective-permute-done.1.k_ref.k_pair.kc, ...), custom_call_target="tpu_custom_call" | custom-call | tf_op jit(solution)/shard_map/pallas_call | solution.py:29
  172.2 2.5 %shard_map.77 = bf16[512,384]{1,0:T(8,128)(2,1)S(1)} custom-call(s32[3]{0:T(128)S(1)} %pad_add_fusion.info_ref, bf16[1024,128]{1,0:T(8,128)(2,1)S(1)} %shard_map.58.refs_0_, bf16[1024,128]{1,0:T(8,128)(2,1)S(1)} %shard_map.61.refs_1_, bf16[1024,128]{1,0:T(8,128)(2,1)S(1)} %shard_map.64.refs_2_, bf16[1024,128]{1,0:T(8,128)(2,1)S(1)} %shard_map.67.refs_3_, ...), custom_call_target="tpu_custom_call" | custom-call | tf_op jit(solution)/shard_map/pallas_call | solution.py:29
  175.9 4.4 %shard_map.78 = (f32[512,256]{1,0:T(8,128)S(1)}, bf16[2,512,1024]{2,1,0:T(8,128)(2,1)S(1)}) custom-call(s32[3]{0:T(128)S(1)} %pad_add_fusion.info_ref, bf16[512,640]{1,0:T(8,128)(2,1)S(1)} %collective-permute-done.qb_ref.q_ref, bf16[512,640]{1,0:T(8,128)(2,1)} %collective-permute-done.1.k_ref.k_pair.kc, ...), custom_call_target="tpu_custom_call" | custom-call | tf_op jit(solution)/shard_map/pallas_call | solution.py:29
  180.4 2.1 %shard_map.79 = bf16[512,256]{1,0:T(8,128)(2,1)S(1)} custom-call(s32[3]{0:T(128)S(1)} %pad_add_fusion.info_ref, bf16[1024,128]{1,0:T(8,128)(2,1)S(1)} %shard_map.58.refs_0_, bf16[1024,128]{1,0:T(8,128)(2,1)S(1)} %shard_map.61.refs_1_, bf16[1024,128]{1,0:T(8,128)(2,1)S(1)} %shard_map.64.refs_2_, bf16[1024,128]{1,0:T(8,128)(2,1)S(1)} %shard_map.67.refs_3_, ...), custom_call_target="tpu_custom_call" | custom-call | tf_op jit(solution)/shard_map/pallas_call | solution.py:29
  183.4 8.1 %shard_map.71 = (f32[512,640]{1,0:T(8,128)S(1)}, bf16[5,512,1024]{2,1,0:T(8,128)(2,1)S(1)}) custom-call(s32[3]{0:T(128)S(1)} %pad_add_fusion.info_ref, bf16[512,640]{1,0:T(8,128)(2,1)S(1)} %copy-done.4, bf16[512,640]{1,0:T(8,128)(2,1)} %shard_map.51.k_ref.kc.k_pair, bf16[512,640]{1,0:T(8,128)(2,1)} %get-tuple-element.57.v_ref.a_ref.vc.v_pair, ...), custom_call_target="tpu_custom_call" | custom-call | tf_op jit(solution)/shard_map/pallas_call | solution.py:29
  191.5 2.3 %shard_map.75.refs_1_ = bf16[512,256]{1,0:T(8,128)(2,1)S(1)} custom-call(s32[3]{0:T(128)S(1)} %pad_add_fusion.info_ref, bf16[1024,128]{1,0:T(8,128)(2,1)S(1)} %shard_map.58.refs_0_, bf16[1024,128]{1,0:T(8,128)(2,1)S(1)} %shard_map.61.refs_1_, bf16[1024,128]{1,0:T(8,128)(2,1)S(1)} %shard_map.64.refs_2_, bf16[1024,128]{1,0:T(8,128)(2,1)S(1)} %shard_map.67.refs_3_, ...), custom_call_target="tpu_custom_call" | custom-call | tf_op jit(solution)/shard_map/pallas_call | solution.py:29
  193.9 2.5 %shard_map.72.refs_0_ = bf16[512,384]{1,0:T(8,128)(2,1)S(1)} custom-call(s32[3]{0:T(128)S(1)} %pad_add_fusion.info_ref, bf16[1024,128]{1,0:T(8,128)(2,1)S(1)} %shard_map.58.refs_0_, bf16[1024,128]{1,0:T(8,128)(2,1)S(1)} %shard_map.61.refs_1_, bf16[1024,128]{1,0:T(8,128)(2,1)S(1)} %shard_map.64.refs_2_, bf16[1024,128]{1,0:T(8,128)(2,1)S(1)} %shard_map.67.refs_3_, ...), custom_call_target="tpu_custom_call" | custom-call | tf_op jit(solution)/shard_map/pallas_call | solution.py:29
  196.4 1.6 shard_map.80
  (79 shorter events, 38.5 us)
Async XLA Ops:
  2.7 21.2 %collective-permute-start.1 = (bf16[512,640]{1,0:T(8,128)(2,1)}, bf16[512,640]{1,0:T(8,128)(2,1)}, u32[]{:S(2)}, u32[]{:S(2)}) collective-permute-start(bf16[512,640]{1,0:T(8,128)(2,1)} %shard_map.47), channel_id=1, source_target_pairs={{0,4},{4,0},{8,12},{12,8},{16,20},{20,16},{24,28},{28,24},{1,5},{5... | collective-permute-start | bytes 1966088 | tf_op jit(solution)/shard_map/ppermute | solution.py:470
  8.8 40.3 %collective-permute-start.2 = (bf16[512,640]{1,0:T(8,128)(2,1)}, bf16[512,640]{1,0:T(8,128)(2,1)}, u32[]{:S(2)}, u32[]{:S(2)}) collective-permute-start(bf16[512,640]{1,0:T(8,128)(2,1)} %get-tuple-element.55), channel_id=1, source_target_pairs={{0,4},{4,0},{8,12},{12,8},{16,20},{20,16},{24,28},{28,24},{1,5},{5... | collective-permute-start | bytes 1966088 | tf_op jit(solution)/shard_map/ppermute | solution.py:470
  12.6 46.9 %collective-permute-start = (bf16[512,640]{1,0:T(8,128)(2,1)}, bf16[512,640]{1,0:T(8,128)(2,1)S(1)}, u32[]{:S(2)}, u32[]{:S(2)}) collective-permute-start(bf16[512,640]{1,0:T(8,128)(2,1)} %get-tuple-element.53), channel_id=1, source_target_pairs={{0,4},{4,0},{8,12},{12,8},{16,20},{20,16},{24,28},{28,24},{1,5},{5... | collective-permute-start | bytes 1966088 | tf_op jit(solution)/shard_map/ppermute | solution.py:470
  17.2 43.6 %collective-permute-start.23 = (bf16[512,640]{1,0:T(8,128)(2,1)}, bf16[512,640]{1,0:T(8,128)(2,1)}, u32[]{:S(2)}, u32[]{:S(2)}) collective-permute-start(bf16[512,640]{1,0:T(8,128)(2,1)} %shard_map.51.k_ref.kc.k_pair), channel_id=1, source_target_pairs={{0,8},{4,12},{8,16},{12,20},{16,24},{20,28},{1,9},{5,13},{9,17},{1... | collective-permute-start | bytes 1966088 | tf_op jit(solution)/shard_map/ppermute | solution.py:470
  21.5 40.6 %collective-permute-start.19 = (bf16[512,640]{1,0:T(8,128)(2,1)}, bf16[512,640]{1,0:T(8,128)(2,1)}, u32[]{:S(2)}, u32[]{:S(2)}) collective-permute-start(bf16[512,640]{1,0:T(8,128)(2,1)} %get-tuple-element.57.v_ref.a_ref.vc.v_pair), channel_id=1, source_target_pairs={{8,16},{12,20},{16,24},{20,28},{9,17},{13,21},{17,25},{21,29},{10,... | collective-permute-start | bytes 1966088 | tf_op jit(solution)/shard_map/ppermute | solution.py:470
  23.8 25.3 %collective-permute-start.3 = (f32[8,512]{1,0:T(8,128)S(1)}, f32[8,512]{1,0:T(8,128)S(1)}, u32[]{:S(2)}, u32[]{:S(2)}) collective-permute-start(f32[8,512]{1,0:T(8,128)S(1)} %get-tuple-element.56), channel_id=1, source_target_pairs={{0,4},{4,0},{8,12},{12,8},{16,20},{20,16},{24,28},{28,24},{1,5},{5... | collective-permute-start | bytes 49160 | tf_op jit(solution)/shard_map/ppermute | solution.py:470
  29.7 21.3 %copy-start.2 = (bf16[2,512,640]{2,1,0:T(8,128)(2,1)S(1)}, bf16[2,512,640]{2,1,0:T(8,128)(2,1)}, u32[]{:S(2)}) copy-start(bf16[2,512,640]{2,1,0:T(8,128)(2,1)} %rest_1_.11) | copy-start | bytes 3932164
  54.4 11.8 %collective-permute-start.10 = (bf16[640,256]{1,0:T(8,128)(2,1)S(1)}, bf16[640,256]{1,0:T(8,128)(2,1)S(1)}, u32[]{:S(2)}, u32[]{:S(2)}) collective-permute-start(bf16[640,256]{1,0:T(8,128)(2,1)S(1)} %get-tuple-element.74), channel_id=1, source_target_pairs={{0,8},{4,12},{24,16},{28,20},{1,9},{5,13},{25,17},{29,21},{2,10},{... | collective-permute-start | bytes 983048 | tf_op jit(solution)/shard_map/ppermute | solution.py:470
  58.1 15.1 %collective-permute-start.7 = (bf16[640,256]{1,0:T(8,128)(2,1)S(1)}, bf16[640,256]{1,0:T(8,128)(2,1)S(1)}, u32[]{:S(2)}, u32[]{:S(2)}) collective-permute-start(bf16[640,256]{1,0:T(8,128)(2,1)S(1)} %get-tuple-element.70), channel_id=1, source_target_pairs={{0,8},{4,12},{24,16},{28,20},{1,9},{5,13},{25,17},{29,21},{2,10},{... | collective-permute-start | bytes 983048 | tf_op jit(solution)/shard_map/ppermute | solution.py:470
  59.4 33.6 %collective-permute-start.16 = (bf16[512,384]{1,0:T(8,128)(2,1)S(1)}, bf16[512,384]{1,0:T(8,128)(2,1)S(1)}, u32[]{:S(2)}, u32[]{:S(2)}) collective-permute-start(bf16[512,384]{1,0:T(8,128)(2,1)S(1)} %get-tuple-element.82), channel_id=1, source_target_pairs={{0,8},{4,12},{24,16},{28,20},{1,9},{5,13},{25,17},{29,21},{2,10},{... | collective-permute-start | bytes 1179656 | tf_op jit(solution)/shard_map/ppermute | solution.py:470
  60.8 27.9 %collective-permute-start.4 = (bf16[640,256]{1,0:T(8,128)(2,1)S(1)}, bf16[640,256]{1,0:T(8,128)(2,1)S(1)}, u32[]{:S(2)}, u32[]{:S(2)}) collective-permute-start(bf16[640,256]{1,0:T(8,128)(2,1)S(1)} %get-tuple-element.65), channel_id=1, source_target_pairs={{0,8},{4,12},{24,16},{28,20},{1,9},{5,13},{25,17},{29,21},{2,10},{... | collective-permute-start | bytes 983048 | tf_op jit(solution)/shard_map/ppermute | solution.py:470
  62.1 39.2 %collective-permute-start.13 = (bf16[1152,256]{1,0:T(8,128)(2,1)S(1)}, bf16[1152,256]{1,0:T(8,128)(2,1)S(1)}, u32[]{:S(2)}, u32[]{:S(2)}) collective-permute-start(bf16[1152,256]{1,0:T(8,128)(2,1)S(1)} %get-tuple-element.78), channel_id=1, source_target_pairs={{0,8},{4,12},{24,16},{28,20},{1,9},{5,13},{25,17},{29,21},{2,10},{... | collective-permute-start | bytes 1769480 | tf_op jit(solution)/shard_map/ppermute | solution.py:470
  66.2 27.8 %collective-permute-start.22 = (bf16[512,384]{1,0:T(8,128)(2,1)S(1)}, bf16[512,384]{1,0:T(8,128)(2,1)S(1)}, u32[]{:S(2)}, u32[]{:S(2)}) collective-permute-start(bf16[512,384]{1,0:T(8,128)(2,1)S(1)} %get-tuple-element.87), channel_id=1, source_target_pairs={{8,16},{12,20},{9,17},{13,21},{10,18},{14,22},{11,19},{15,23}} | collective-permute-start | bytes 1179656 | tf_op jit(solution)/shard_map/ppermute | solution.py:470
  73.2 28.8 %collective-permute-start.11 = (bf16[640,256]{1,0:T(8,128)(2,1)S(1)}, bf16[640,256]{1,0:T(8,128)(2,1)S(1)}, u32[]{:S(2)}, u32[]{:S(2)}) collective-permute-start(bf16[640,256]{1,0:T(8,128)(2,1)S(1)} %get-tuple-element.76), channel_id=1, source_target_pairs={{8,16},{12,20},{16,8},{20,12},{9,17},{13,21},{17,9},{21,13},{10,18... | collective-permute-start | bytes 983048 | tf_op jit(solution)/shard_map/ppermute | solution.py:470
  88.6 39.7 %collective-permute-start.24 = (bf16[512,640]{1,0:T(8,128)(2,1)}, bf16[512,640]{1,0:T(8,128)(2,1)S(1)}, u32[]{:S(2)}, u32[]{:S(2)}) collective-permute-start(bf16[512,640]{1,0:T(8,128)(2,1)} %collective-permute-done.1.k_ref.k_pair.kc), channel_id=1, source_target_pairs={{0,8},{4,12},{8,16},{12,20},{16,24},{20,28},{1,9},{5,13},{9,17},{1... | collective-permute-start | bytes 1966088 | tf_op jit(solution)/shard_map/ppermute | solution.py:470
  93.1 36.6 %collective-permute-start.21 = (bf16[512,640]{1,0:T(8,128)(2,1)}, bf16[512,640]{1,0:T(8,128)(2,1)S(1)}, u32[]{:S(2)}, u32[]{:S(2)}) collective-permute-start(bf16[512,640]{1,0:T(8,128)(2,1)} %collective-permute-done.2.v_ref.b_ref.v_pair.vc), channel_id=1, source_target_pairs={{16,24},{20,28},{17,25},{21,29},{18,26},{22,30},{19,27},{23,31}} | collective-permute-start | bytes 1966088 | tf_op jit(solution)/shard_map/ppermute | solution.py:470
  94.0 8.8 %collective-permute-start.8 = (bf16[640,256]{1,0:T(8,128)(2,1)S(1)}, bf16[640,256]{1,0:T(8,128)(2,1)S(1)}, u32[]{:S(2)}, u32[]{:S(2)}) collective-permute-start(bf16[640,256]{1,0:T(8,128)(2,1)S(1)} %get-tuple-element.72), channel_id=1, source_target_pairs={{8,16},{12,20},{16,8},{20,12},{9,17},{13,21},{17,9},{21,13},{10,18... | collective-permute-start | bytes 983048 | tf_op jit(solution)/shard_map/ppermute | solution.py:470
  101.3 2.2 %collective-permute-start.5 = (bf16[640,256]{1,0:T(8,128)(2,1)S(1)}, bf16[640,256]{1,0:T(8,128)(2,1)S(1)}, u32[]{:S(2)}, u32[]{:S(2)}) collective-permute-start(bf16[640,256]{1,0:T(8,128)(2,1)S(1)} %get-tuple-element.67), channel_id=1, source_target_pairs={{8,16},{12,20},{16,8},{20,12},{9,17},{13,21},{17,9},{21,13},{10,18... | collective-permute-start | bytes 983048 | tf_op jit(solution)/shard_map/ppermute | solution.py:470
  102.0 28.4 %collective-permute-start.17 = (bf16[512,384]{1,0:T(8,128)(2,1)S(1)}, bf16[512,384]{1,0:T(8,128)(2,1)S(1)}, u32[]{:S(2)}, u32[]{:S(2)}) collective-permute-start(bf16[512,384]{1,0:T(8,128)(2,1)S(1)} %get-tuple-element.84), channel_id=1, source_target_pairs={{8,16},{12,20},{16,8},{20,12},{9,17},{13,21},{17,9},{21,13},{10,18... | collective-permute-start | bytes 1179656 | tf_op jit(solution)/shard_map/ppermute | solution.py:470
  102.7 29.7 %collective-permute-start.14 = (bf16[640,256]{1,0:T(8,128)(2,1)S(1)}, bf16[640,256]{1,0:T(8,128)(2,1)S(1)}, u32[]{:S(2)}, u32[]{:S(2)}) collective-permute-start(bf16[640,256]{1,0:T(8,128)(2,1)S(1)} %get-tuple-element.80), channel_id=1, source_target_pairs={{8,16},{12,20},{16,8},{20,12},{9,17},{13,21},{17,9},{21,13},{10,18... | collective-permute-start | bytes 983048 | tf_op jit(solution)/shard_map/ppermute | solution.py:470
  103.4 68.8 %collective-permute-start.20 = (bf16[2,512,384]{2,1,0:T(8,128)(2,1)S(1)}, bf16[2,512,384]{2,1,0:T(8,128)(2,1)S(1)}, u32[]{:S(2)}, u32[]{:S(2)}) collective-permute-start(bf16[2,512,384]{2,1,0:T(8,128)(2,1)S(1)} %get-tuple-element.86), channel_id=1, source_target_pairs={{0,8},{4,12},{1,9},{5,13},{2,10},{6,14},{3,11},{7,15}} | collective-permute-start | bytes 2359304 | tf_op jit(solution)/shard_map/ppermute | solution.py:470
  128.3 12.5 %collective-permute-start.12 = (bf16[640,256]{1,0:T(8,128)(2,1)S(1)}, bf16[640,256]{1,0:T(8,128)(2,1)S(1)}, u32[]{:S(2)}, u32[]{:S(2)}) collective-permute-start(bf16[640,256]{1,0:T(8,128)(2,1)S(1)} %shard_map.63.made_ref), channel_id=1, source_target_pairs={{8,0},{12,4},{16,24},{20,28},{9,1},{13,5},{17,25},{21,29},{10,2},{... | collective-permute-start | bytes 983048 | tf_op jit(solution)/shard_map/ppermute | solution.py:470
  129.7 4.9 %collective-permute-start.25 = (bf16[512,256]{1,0:T(8,128)(2,1)S(1)}, bf16[512,256]{1,0:T(8,128)(2,1)S(1)}, u32[]{:S(2)}, u32[]{:S(2)}) collective-permute-start(bf16[512,256]{1,0:T(8,128)(2,1)S(1)} %get-tuple-element.92), channel_id=1, source_target_pairs={{8,16},{12,20},{16,8},{20,12},{9,17},{13,21},{17,9},{21,13},{10,18... | collective-permute-start | bytes 786440 | tf_op jit(solution)/shard_map/ppermute | solution.py:470
  130.3 17.5 %collective-permute-start.9 = (bf16[640,256]{1,0:T(8,128)(2,1)S(1)}, bf16[640,256]{1,0:T(8,128)(2,1)S(1)}, u32[]{:S(2)}, u32[]{:S(2)}) collective-permute-start(bf16[640,256]{1,0:T(8,128)(2,1)S(1)} %shard_map.60.made_ref), channel_id=1, source_target_pairs={{8,0},{12,4},{16,24},{20,28},{9,1},{13,5},{17,25},{21,29},{10,2},{... | collective-permute-start | bytes 983048 | tf_op jit(solution)/shard_map/ppermute | solution.py:470
  132.5 22.4 %collective-permute-start.6 = (bf16[640,256]{1,0:T(8,128)(2,1)S(1)}, bf16[640,256]{1,0:T(8,128)(2,1)S(1)}, u32[]{:S(2)}, u32[]{:S(2)}) collective-permute-start(bf16[640,256]{1,0:T(8,128)(2,1)S(1)} %shard_map.57.made_ref), channel_id=1, source_target_pairs={{8,0},{12,4},{16,24},{20,28},{9,1},{13,5},{17,25},{21,29},{10,2},{... | collective-permute-start | bytes 983048 | tf_op jit(solution)/shard_map/ppermute | solution.py:470
  134.6 25.9 %collective-permute-start.15 = (bf16[640,256]{1,0:T(8,128)(2,1)S(1)}, bf16[640,256]{1,0:T(8,128)(2,1)S(1)}, u32[]{:S(2)}, u32[]{:S(2)}) collective-permute-start(bf16[640,256]{1,0:T(8,128)(2,1)S(1)} %shard_map.66.made_ref), channel_id=1, source_target_pairs={{8,0},{12,4},{16,24},{20,28},{9,1},{13,5},{17,25},{21,29},{10,2},{... | collective-permute-start | bytes 983048 | tf_op jit(solution)/shard_map/ppermute | solution.py:470
  140.8 39.5 %collective-permute-start.27 = (bf16[2,512,256]{2,1,0:T(8,128)(2,1)S(1)}, bf16[2,512,256]{2,1,0:T(8,128)(2,1)S(1)}, u32[]{:S(2)}, u32[]{:S(2)}) collective-permute-start(bf16[2,512,256]{2,1,0:T(8,128)(2,1)S(1)} %get-tuple-element.93), channel_id=1, source_target_pairs={{0,8},{4,12},{1,9},{5,13},{2,10},{6,14},{3,11},{7,15}} | collective-permute-start | bytes 1572872 | tf_op jit(solution)/shard_map/ppermute | solution.py:470
  147.8 24.4 %collective-permute-start.18 = (bf16[512,384]{1,0:T(8,128)(2,1)S(1)}, bf16[512,384]{1,0:T(8,128)(2,1)S(1)}, u32[]{:S(2)}, u32[]{:S(2)}) collective-permute-start(bf16[512,384]{1,0:T(8,128)(2,1)S(1)} %shard_map.69.refs_4_), channel_id=1, source_target_pairs={{8,0},{12,4},{16,24},{20,28},{9,1},{13,5},{17,25},{21,29},{10,2},{... | collective-permute-start | bytes 1179656 | tf_op jit(solution)/shard_map/ppermute | solution.py:470
  154.9 25.5 %collective-permute-start.28 = (bf16[512,256]{1,0:T(8,128)(2,1)S(1)}, bf16[512,256]{1,0:T(8,128)(2,1)S(1)}, u32[]{:S(2)}, u32[]{:S(2)}) collective-permute-start(bf16[512,256]{1,0:T(8,128)(2,1)S(1)} %get-tuple-element.94), channel_id=1, source_target_pairs={{8,16},{12,20},{9,17},{13,21},{10,18},{14,22},{11,19},{15,23}} | collective-permute-start | bytes 786440 | tf_op jit(solution)/shard_map/ppermute | solution.py:470
  160.5 19.9 %collective-permute-start.26 = (bf16[512,256]{1,0:T(8,128)(2,1)S(1)}, bf16[512,256]{1,0:T(8,128)(2,1)S(1)}, u32[]{:S(2)}, u32[]{:S(2)}) collective-permute-start(bf16[512,256]{1,0:T(8,128)(2,1)S(1)} %shard_map.74.refs_4_), channel_id=1, source_target_pairs={{8,0},{12,4},{16,24},{20,28},{9,1},{13,5},{17,25},{21,29},{10,2},{... | collective-permute-start | bytes 786440 | tf_op jit(solution)/shard_map/ppermute | solution.py:470
  174.8 21.6 %collective-permute-start.29 = (bf16[512,384]{1,0:T(8,128)(2,1)S(1)}, bf16[512,384]{1,0:T(8,128)(2,1)S(1)}, u32[]{:S(2)}, u32[]{:S(2)}) collective-permute-start(bf16[512,384]{1,0:T(8,128)(2,1)S(1)} %shard_map.77), channel_id=1, source_target_pairs={{0,4},{4,0},{8,12},{12,8},{16,20},{20,16},{24,28},{28,24},{1,5},{5... | collective-permute-start | bytes 1179656 | tf_op jit(solution)/shard_map/ppermute | solution.py:470
  182.5 13.9 %collective-permute-start.30 = (bf16[512,256]{1,0:T(8,128)(2,1)S(1)}, bf16[512,256]{1,0:T(8,128)(2,1)S(1)}, u32[]{:S(2)}, u32[]{:S(2)}) collective-permute-start(bf16[512,256]{1,0:T(8,128)(2,1)S(1)} %shard_map.79), channel_id=1, source_target_pairs={{0,4},{4,0},{8,12},{12,8},{16,20},{20,16},{24,28},{28,24},{1,5},{5... | collective-permute-start | bytes 786440 | tf_op jit(solution)/shard_map/ppermute | solution.py:470
  (5 other events, 42.2 us)

commit v3 on v2

--- a/solution.py
+++ b/solution.py
@@ -12,7 +12,7 @@
 EPS = 1e-06
 F32 = jnp.float32
 BF16 = jnp.bfloat16
-PIECES = 4
+PIECES = 1
 VMEM_LIMIT = 20 * 1024 * 1024
 
 
@@ -539,7 +539,8 @@
     heads = head_width // ADIM
     split = middle // ADIM
     blocks = (k_own, v_own, k_oth, v_oth, pk_own, pk_oth)
-    own_sum, own_p = attention(info, 0, (0, heads), q_own, *blocks)
+    own_some = attention(info, 0, (0, split), q_own, *blocks)
+    own_rest = attention(info, 0, (split, heads), q_own, *blocks)
     oth_some = attention(info, 1, (0, split), q_oth, *blocks)
     oth_rest = attention(info, 1, (split, heads), q_oth, *blocks)
     hiddens = [query_hidden(info, q_own, q_oth, made[i], got[i]) for i in range(1, 1 + parts)]
@@ -547,13 +548,13 @@
     for i, (lo, hi) in enumerate(out_cuts):
         at = parts + i if i else 0
         some = (hiddens, made[at], got[at])
-        if lo < middle:
-            left = (oth_some[0], lo, oth_some[1])
-        else:
-            left = (oth_rest[0], lo - middle, oth_rest[1])
+        first, place = lo < middle, lo if lo < middle else lo - middle
+        own_left = own_some if first else own_rest
+        oth_left = oth_some if first else oth_rest
+        left = (oth_left[0], place, oth_left[1])
         theirs = apply_chunk(info, 1, *some, left, late_vals[i], lo, hi)
         oth_parts.append(permute(theirs, swap_pairs))
-        left = (own_sum, lo, own_p)
+        left = (own_left[0], place, own_left[1])
         own_parts.append(apply_chunk(info, 0, *some, left, late_vals[i], lo, hi))
     return assemble(info, own_parts, oth_parts, out_cuts)
 

time: 199 us -> 202 us (1.015)
    pallas_call x35 -> x36, Pallas kernels: 64.5 us -> 66.5 us  [call(): pl.pallas_call(body, in_specs=ins, out_specs=out_specs if out_specs is no...]
  transfers between devices with their start and end apart: 31 -> 31, of which waited for: 9 -> 9; matrix products, arithmetic and copies ran while one was open for 0% -> 0% of each run, Pallas kernels for 30% -> 31%
where the time goes in v3:
time: 202 us; the launch traced here: 201 us
  starting transfers between devices  67.2 us (33%)
  Pallas kernels  66.5 us (33%)
  waiting for transfers between devices  64.1 us (32%)
  local copies, waits for them, and re-layouts  2.34 us (1%)
    ppermute x31, starting transfers between devices, permute(): return lax.ppermute(array, 'ctx', pairs)  67.2 us
    pallas_call x36, Pallas kernels, call(): pl.pallas_call(body, in_specs=ins, out_specs=out_specs if out_specs is no...  66.5 us
    ppermute x31, waiting for transfers between devices, permute(): return lax.ppermute(array, 'ctx', pairs)  64.1 us
  transfers between devices with their start and end apart: 31, of which 9 were waited for; matrix products, arithmetic and copies ran while one was open for 0% of the time, Pallas kernels for 31%

profile of v3, /device:TPU:0, one launch (start us, length us, event | category | flops | bytes accessed | tf_op | source)
XLA Modules:
  0.0 201.1 jit_solution(1612649613381942830)
XLA Ops:
  0.1 2.5 %shard_map.47 = bf16[512,640]{1,0:T(8,128)(2,1)} custom-call(s32[3]{0:T(128)S(1)} %pad_add_fusion.info_ref, bf16[3,512,1280]{2,1,0:T(8,128)(2,1)} %qkv_ref.7), custom_call_target="tpu_custom_call" | custom-call | tf_op jit(solution)/shard_map/pallas_call | solution.py:29
  2.6 3.1 %collective-permute-start.1 = (bf16[512,640]{1,0:T(8,128)(2,1)}, bf16[512,640]{1,0:T(8,128)(2,1)S(1)}, u32[]{:S(2)}, u32[]{:S(2)}) collective-permute-start(bf16[512,640]{1,0:T(8,128)(2,1)} %shard_map.47), channel_id=1, source_target_pairs={{0,4},{4,0},{8,12},{12,8},{16,20},{20,16},{24,28},{28,24},{1,5},{5... | collective-permute-start | bytes 1966088 | tf_op jit(solution)/shard_map/ppermute | solution.py:470
  5.6 2.9 %shard_map.49 = (bf16[512,640]{1,0:T(8,128)(2,1)}, bf16[512,640]{1,0:T(8,128)(2,1)}) custom-call(s32[3]{0:T(128)S(1)} %pad_add_fusion.info_ref, bf16[3,512,1280]{2,1,0:T(8,128)(2,1)} %qkv_ref.7), custom_call_target="tpu_custom_call" | custom-call | tf_op jit(solution)/shard_map/pallas_call | solution.py:29
  8.6 2.7 %shard_map.46 = (bf16[512,640]{1,0:T(8,128)(2,1)}, bf16[512,640]{1,0:T(8,128)(2,1)S(1)}) custom-call(s32[3]{0:T(128)S(1)} %pad_add_fusion.info_ref, bf16[3,512,1280]{2,1,0:T(8,128)(2,1)} %qkv_ref.7), custom_call_target="tpu_custom_call" | custom-call | tf_op jit(solution)/shard_map/pallas_call | solution.py:29
  12.2 2.0 collective-permute-start
  14.2 2.5 %shard_map.51.k_ref.kc.k_pair = bf16[512,640]{1,0:T(8,128)(2,1)} custom-call(s32[3]{0:T(128)S(1)} %pad_add_fusion.info_ref, bf16[3,512,1280]{2,1,0:T(8,128)(2,1)} %qkv_ref.7), custom_call_target="tpu_custom_call" | custom-call | tf_op jit(solution)/shard_map/pallas_call | solution.py:29
  16.7 4.3 %collective-permute-start.23 = (bf16[512,640]{1,0:T(8,128)(2,1)}, bf16[512,640]{1,0:T(8,128)(2,1)}, u32[]{:S(2)}, u32[]{:S(2)}) collective-permute-start(bf16[512,640]{1,0:T(8,128)(2,1)} %shard_map.51.k_ref.kc.k_pair), channel_id=1, source_target_pairs={{0,8},{4,12},{8,16},{12,20},{16,24},{20,28},{1,9},{5,13},{9,17},{1... | collective-permute-start | bytes 1966088 | tf_op jit(solution)/shard_map/ppermute | solution.py:470
  25.2 4.0 %shard_map.52 = (f32[640,1024]{1,0:T(8,128)S(1)}, f32[512,640]{1,0:T(8,128)S(1)}) custom-call(s32[3]{0:T(128)S(1)} %pad_add_fusion.info_ref, bf16[512,640]{1,0:T(8,128)(2,1)} %shard_map.51.k_ref.kc.k_pair, bf16[512,640]{1,0:T(8,128)(2,1)} %get-tuple-element.59.v_ref.a_ref.vc.v_pair, f32[8,512]{1,0:T(8,128)S(1)} %get-tuple-element.60.rate_ref, ...), custom_call_target="tpu_custom_call" | custom-call | tf_op jit(solution)/shard_map/pallas_call | solution.py:29
  29.2 1.7 shard_map.48
  30.9 18.1 %collective-permute-done.3.rate_ref = f32[8,512]{1,0:T(8,128)S(1)} collective-permute-done((f32[8,512]{1,0:T(8,128)S(1)}, f32[8,512]{1,0:T(8,128)S(1)}, u32[]{:S(2)}, u32[]{:S(2)}) %collective-permute-start.3) | collective-permute-done | bytes 16416 | tf_op jit(solution)/shard_map/ppermute | solution.py:470
  49.0 1.8 shard_map.53
  50.9 2.8 %shard_map.54 = (bf16[640,256]{1,0:T(8,128)(2,1)S(1)}, bf16[640,256]{1,0:T(8,128)(2,1)S(1)}, bf16[640,256]{1,0:T(8,128)(2,1)S(1)}, bf16[1152,256]{1,0:T(8,128)(2...) custom-call(s32[3]{0:T(128)S(1)} %pad_add_fusion.info_ref, ...), custom_call_target="tpu_custom_call" | custom-call | tf_op jit(solution)/shard_map/pallas_call | solution.py:29
  53.7 3.7 %collective-permute-start.10 = (bf16[640,256]{1,0:T(8,128)(2,1)S(1)}, bf16[640,256]{1,0:T(8,128)(2,1)S(1)}, u32[]{:S(2)}, u32[]{:S(2)}) collective-permute-start(bf16[640,256]{1,0:T(8,128)(2,1)S(1)} %get-tuple-element.76), channel_id=1, source_target_pairs={{0,8},{4,12},{24,16},{28,20},{1,9},{5,13},{25,17},{29,21},{2,10},{... | collective-permute-start | bytes 983048 | tf_op jit(solution)/shard_map/ppermute | solution.py:470
  66.3 6.3 %collective-permute-done.7.got_ref = bf16[640,256]{1,0:T(8,128)(2,1)S(1)} collective-permute-done((bf16[640,256]{1,0:T(8,128)(2,1)S(1)}, bf16[640,256]{1,0:T(8,128)(2,1)S(1)}, u32[]{:S(2)}, u32[]{:S(2)}) %collective-permute-start.7) | collective-permute-done | bytes 327712 | tf_op jit(solution)/shard_map/ppermute | solution.py:470
  73.2 14.8 %collective-permute-done.4.got_ref = bf16[640,256]{1,0:T(8,128)(2,1)S(1)} collective-permute-done((bf16[640,256]{1,0:T(8,128)(2,1)S(1)}, bf16[640,256]{1,0:T(8,128)(2,1)S(1)}, u32[]{:S(2)}, u32[]{:S(2)}) %collective-permute-start.4) | collective-permute-done | bytes 327712 | tf_op jit(solution)/shard_map/ppermute | solution.py:470
  88.0 4.4 %collective-permute-start.24 = (bf16[512,640]{1,0:T(8,128)(2,1)S(1)}, bf16[512,640]{1,0:T(8,128)(2,1)S(1)}, u32[]{:S(2)}, u32[]{:S(2)}) collective-permute-start(bf16[512,640]{1,0:T(8,128)(2,1)S(1)} %collective-permute-done.1.k_ref.k_pair.kc), channel_id=1, source_target_pairs={{0,8},{4,12},{8,16},{12,20},{16,24},{20,28},{1,9},{5,13},{9,17},{1... | collective-permute-start | bytes 1966088 | tf_op jit(solution)/shard_map/ppermute | solution.py:470
  94.1 6.5 %collective-permute-done.13.got_ref = bf16[1152,256]{1,0:T(8,128)(2,1)S(1)} collective-permute-done((bf16[1152,256]{1,0:T(8,128)(2,1)S(1)}, bf16[1152,256]{1,0:T(8,128)(2,1)S(1)}, u32[]{:S(2)}, u32[]{:S(2)}) %collective-permute-start.13) | collective-permute-done | bytes 589856 | tf_op jit(solution)/shard_map/ppermute | solution.py:470
  102.8 22.2 %collective-permute-start.20 = (bf16[2,512,384]{2,1,0:T(8,128)(2,1)S(1)}, bf16[2,512,384]{2,1,0:T(8,128)(2,1)S(1)}, u32[]{:S(2)}, u32[]{:S(2)}) collective-permute-start(bf16[2,512,384]{2,1,0:T(8,128)(2,1)S(1)} %get-tuple-element.88), channel_id=1, source_target_pairs={{0,8},{4,12},{1,9},{5,13},{2,10},{6,14},{3,11},{7,15}} | collective-permute-start | bytes 2359304 | tf_op jit(solution)/shard_map/ppermute | solution.py:470
  135.9 4.1 %collective-permute-done.12.got_ref = bf16[640,256]{1,0:T(8,128)(2,1)S(1)} collective-permute-done((bf16[640,256]{1,0:T(8,128)(2,1)S(1)}, bf16[640,256]{1,0:T(8,128)(2,1)S(1)}, u32[]{:S(2)}, u32[]{:S(2)}) %collective-permute-start.12) | collective-permute-done | bytes 327712 | tf_op jit(solution)/shard_map/ppermute | solution.py:470
  140.0 3.9 %collective-permute-start.27 = (bf16[2,512,256]{2,1,0:T(8,128)(2,1)S(1)}, bf16[2,512,256]{2,1,0:T(8,128)(2,1)S(1)}, u32[]{:S(2)}, u32[]{:S(2)}) collective-permute-start(bf16[2,512,256]{2,1,0:T(8,128)(2,1)S(1)} %get-tuple-element.95), channel_id=1, source_target_pairs={{0,8},{4,12},{1,9},{5,13},{2,10},{6,14},{3,11},{7,15}} | collective-permute-start | bytes 1572872 | tf_op jit(solution)/shard_map/ppermute | solution.py:470
  143.9 3.1 %collective-permute-done.9.got_ref = bf16[640,256]{1,0:T(8,128)(2,1)S(1)} collective-permute-done((bf16[640,256]{1,0:T(8,128)(2,1)S(1)}, bf16[640,256]{1,0:T(8,128)(2,1)S(1)}, u32[]{:S(2)}, u32[]{:S(2)}) %collective-permute-start.9) | collective-permute-done | bytes 327712 | tf_op jit(solution)/shard_map/ppermute | solution.py:470
  149.0 5.0 %collective-permute-done.6.got_ref = bf16[640,256]{1,0:T(8,128)(2,1)S(1)} collective-permute-done((bf16[640,256]{1,0:T(8,128)(2,1)S(1)}, bf16[640,256]{1,0:T(8,128)(2,1)S(1)}, u32[]{:S(2)}, u32[]{:S(2)}) %collective-permute-start.6) | collective-permute-done | bytes 327712 | tf_op jit(solution)/shard_map/ppermute | solution.py:470
  154.7 4.9 %collective-permute-done.15.got_ref = bf16[640,256]{1,0:T(8,128)(2,1)S(1)} collective-permute-done((bf16[640,256]{1,0:T(8,128)(2,1)S(1)}, bf16[640,256]{1,0:T(8,128)(2,1)S(1)}, u32[]{:S(2)}, u32[]{:S(2)}) %collective-permute-start.15) | collective-permute-done | bytes 327712 | tf_op jit(solution)/shard_map/ppermute | solution.py:470
  161.1 5.7 %shard_map.77 = (f32[512,384]{1,0:T(8,128)S(1)}, bf16[3,512,1024]{2,1,0:T(8,128)(2,1)S(1)}) custom-call(s32[3]{0:T(128)S(1)} %pad_add_fusion.info_ref, bf16[512,640]{1,0:T(8,128)(2,1)} %collective-permute-done.qb_ref.q_ref, bf16[512,640]{1,0:T(8,128)(2,1)S(1)} %collective-permute-done.1.k_ref.k_pair.kc, ...), custom_call_target="tpu_custom_call" | custom-call | tf_op jit(solution)/shard_map/pallas_call | solution.py:29
  171.9 1.7 shard_map.67.refs_3_
  173.6 2.5 %shard_map.78 = bf16[512,384]{1,0:T(8,128)(2,1)S(1)} custom-call(s32[3]{0:T(128)S(1)} %pad_add_fusion.info_ref, bf16[1024,128]{1,0:T(8,128)(2,1)S(1)} %shard_map.58.refs_0_, bf16[1024,128]{1,0:T(8,128)(2,1)S(1)} %shard_map.61.refs_1_, bf16[1024,128]{1,0:T(8,128)(2,1)S(1)} %shard_map.64.refs_2_, bf16[1024,128]{1,0:T(8,128)(2,1)S(1)} %shard_map.67.refs_3_, ...), custom_call_target="tpu_custom_call" | custom-call | tf_op jit(solution)/shard_map/pallas_call | solution.py:29
  177.7 4.4 %shard_map.79 = (f32[512,256]{1,0:T(8,128)S(1)}, bf16[2,512,1024]{2,1,0:T(8,128)(2,1)S(1)}) custom-call(s32[3]{0:T(128)S(1)} %pad_add_fusion.info_ref, bf16[512,640]{1,0:T(8,128)(2,1)} %collective-permute-done.qb_ref.q_ref, bf16[512,640]{1,0:T(8,128)(2,1)S(1)} %collective-permute-done.1.k_ref.k_pair.kc, ...), custom_call_target="tpu_custom_call" | custom-call | tf_op jit(solution)/shard_map/pallas_call | solution.py:29
  182.2 2.1 %shard_map.80 = bf16[512,256]{1,0:T(8,128)(2,1)S(1)} custom-call(s32[3]{0:T(128)S(1)} %pad_add_fusion.info_ref, bf16[1024,128]{1,0:T(8,128)(2,1)S(1)} %shard_map.58.refs_0_, bf16[1024,128]{1,0:T(8,128)(2,1)S(1)} %shard_map.61.refs_1_, bf16[1024,128]{1,0:T(8,128)(2,1)S(1)} %shard_map.64.refs_2_, bf16[1024,128]{1,0:T(8,128)(2,1)S(1)} %shard_map.67.refs_3_, ...), custom_call_target="tpu_custom_call" | custom-call | tf_op jit(solution)/shard_map/pallas_call | solution.py:29
  184.8 4.2 %shard_map.75 = (f32[512,256]{1,0:T(8,128)S(1)}, bf16[2,512,1024]{2,1,0:T(8,128)(2,1)S(1)}) custom-call(s32[3]{0:T(128)S(1)} %pad_add_fusion.info_ref, bf16[512,640]{1,0:T(8,128)(2,1)S(1)} %copy-done.4, bf16[512,640]{1,0:T(8,128)(2,1)} %shard_map.51.k_ref.kc.k_pair, bf16[512,640]{1,0:T(8,128)(2,1)} %get-tuple-element.59.v_ref.a_ref.vc.v_pair, ...), custom_call_target="tpu_custom_call" | custom-call | tf_op jit(solution)/shard_map/pallas_call | solution.py:29
  189.0 5.4 %shard_map.71 = (f32[512,384]{1,0:T(8,128)S(1)}, bf16[3,512,1024]{2,1,0:T(8,128)(2,1)S(1)}) custom-call(s32[3]{0:T(128)S(1)} %pad_add_fusion.info_ref, bf16[512,640]{1,0:T(8,128)(2,1)S(1)} %copy-done.4, bf16[512,640]{1,0:T(8,128)(2,1)} %shard_map.51.k_ref.kc.k_pair, bf16[512,640]{1,0:T(8,128)(2,1)} %get-tuple-element.59.v_ref.a_ref.vc.v_pair, ...), custom_call_target="tpu_custom_call" | custom-call | tf_op jit(solution)/shard_map/pallas_call | solution.py:29
  194.4 2.3 %shard_map.76.refs_1_ = bf16[512,256]{1,0:T(8,128)(2,1)S(1)} custom-call(s32[3]{0:T(128)S(1)} %pad_add_fusion.info_ref, bf16[1024,128]{1,0:T(8,128)(2,1)S(1)} %shard_map.58.refs_0_, bf16[1024,128]{1,0:T(8,128)(2,1)S(1)} %shard_map.61.refs_1_, bf16[1024,128]{1,0:T(8,128)(2,1)S(1)} %shard_map.64.refs_2_, bf16[1024,128]{1,0:T(8,128)(2,1)S(1)} %shard_map.67.refs_3_, ...), custom_call_target="tpu_custom_call" | custom-call | tf_op jit(solution)/shard_map/pallas_call | solution.py:29
  196.7 2.5 %shard_map.72.refs_0_ = bf16[512,384]{1,0:T(8,128)(2,1)S(1)} custom-call(s32[3]{0:T(128)S(1)} %pad_add_fusion.info_ref, bf16[1024,128]{1,0:T(8,128)(2,1)S(1)} %shard_map.58.refs_0_, bf16[1024,128]{1,0:T(8,128)(2,1)S(1)} %shard_map.61.refs_1_, bf16[1024,128]{1,0:T(8,128)(2,1)S(1)} %shard_map.64.refs_2_, bf16[1024,128]{1,0:T(8,128)(2,1)S(1)} %shard_map.67.refs_3_, ...), custom_call_target="tpu_custom_call" | custom-call | tf_op jit(solution)/shard_map/pallas_call | solution.py:29
  (80 shorter events, 42.1 us)
Async XLA Ops:
  2.6 20.8 %collective-permute-start.1 = (bf16[512,640]{1,0:T(8,128)(2,1)}, bf16[512,640]{1,0:T(8,128)(2,1)S(1)}, u32[]{:S(2)}, u32[]{:S(2)}) collective-permute-start(bf16[512,640]{1,0:T(8,128)(2,1)} %shard_map.47), channel_id=1, source_target_pairs={{0,4},{4,0},{8,12},{12,8},{16,20},{20,16},{24,28},{28,24},{1,5},{5... | collective-permute-start | bytes 1966088 | tf_op jit(solution)/shard_map/ppermute | solution.py:470
  8.6 40.5 %collective-permute-start.2 = (bf16[512,640]{1,0:T(8,128)(2,1)}, bf16[512,640]{1,0:T(8,128)(2,1)}, u32[]{:S(2)}, u32[]{:S(2)}) collective-permute-start(bf16[512,640]{1,0:T(8,128)(2,1)} %get-tuple-element.57), channel_id=1, source_target_pairs={{0,4},{4,0},{8,12},{12,8},{16,20},{20,16},{24,28},{28,24},{1,5},{5... | collective-permute-start | bytes 1966088 | tf_op jit(solution)/shard_map/ppermute | solution.py:470
  12.2 46.6 %collective-permute-start = (bf16[512,640]{1,0:T(8,128)(2,1)}, bf16[512,640]{1,0:T(8,128)(2,1)}, u32[]{:S(2)}, u32[]{:S(2)}) collective-permute-start(bf16[512,640]{1,0:T(8,128)(2,1)} %get-tuple-element.55), channel_id=1, source_target_pairs={{0,4},{4,0},{8,12},{12,8},{16,20},{20,16},{24,28},{28,24},{1,5},{5... | collective-permute-start | bytes 1966088 | tf_op jit(solution)/shard_map/ppermute | solution.py:470
  16.7 43.4 %collective-permute-start.23 = (bf16[512,640]{1,0:T(8,128)(2,1)}, bf16[512,640]{1,0:T(8,128)(2,1)}, u32[]{:S(2)}, u32[]{:S(2)}) collective-permute-start(bf16[512,640]{1,0:T(8,128)(2,1)} %shard_map.51.k_ref.kc.k_pair), channel_id=1, source_target_pairs={{0,8},{4,12},{8,16},{12,20},{16,24},{20,28},{1,9},{5,13},{9,17},{1... | collective-permute-start | bytes 1966088 | tf_op jit(solution)/shard_map/ppermute | solution.py:470
  21.0 40.4 %collective-permute-start.19 = (bf16[512,640]{1,0:T(8,128)(2,1)}, bf16[512,640]{1,0:T(8,128)(2,1)}, u32[]{:S(2)}, u32[]{:S(2)}) collective-permute-start(bf16[512,640]{1,0:T(8,128)(2,1)} %get-tuple-element.59.v_ref.a_ref.vc.v_pair), channel_id=1, source_target_pairs={{8,16},{12,20},{16,24},{20,28},{9,17},{13,21},{17,25},{21,29},{10,... | collective-permute-start | bytes 1966088 | tf_op jit(solution)/shard_map/ppermute | solution.py:470
  23.4 25.7 %collective-permute-start.3 = (f32[8,512]{1,0:T(8,128)S(1)}, f32[8,512]{1,0:T(8,128)S(1)}, u32[]{:S(2)}, u32[]{:S(2)}) collective-permute-start(f32[8,512]{1,0:T(8,128)S(1)} %get-tuple-element.58), channel_id=1, source_target_pairs={{0,4},{4,0},{8,12},{12,8},{16,20},{20,16},{24,28},{28,24},{1,5},{5... | collective-permute-start | bytes 49160 | tf_op jit(solution)/shard_map/ppermute | solution.py:470
  29.2 21.7 %copy-start.2 = (bf16[2,512,640]{2,1,0:T(8,128)(2,1)S(1)}, bf16[2,512,640]{2,1,0:T(8,128)(2,1)}, u32[]{:S(2)}) copy-start(bf16[2,512,640]{2,1,0:T(8,128)(2,1)} %rest_1_.11) | copy-start | bytes 3932164
  53.7 11.8 %collective-permute-start.10 = (bf16[640,256]{1,0:T(8,128)(2,1)S(1)}, bf16[640,256]{1,0:T(8,128)(2,1)S(1)}, u32[]{:S(2)}, u32[]{:S(2)}) collective-permute-start(bf16[640,256]{1,0:T(8,128)(2,1)S(1)} %get-tuple-element.76), channel_id=1, source_target_pairs={{0,8},{4,12},{24,16},{28,20},{1,9},{5,13},{25,17},{29,21},{2,10},{... | collective-permute-start | bytes 983048 | tf_op jit(solution)/shard_map/ppermute | solution.py:470
  57.5 15.1 %collective-permute-start.7 = (bf16[640,256]{1,0:T(8,128)(2,1)S(1)}, bf16[640,256]{1,0:T(8,128)(2,1)S(1)}, u32[]{:S(2)}, u32[]{:S(2)}) collective-permute-start(bf16[640,256]{1,0:T(8,128)(2,1)S(1)} %get-tuple-element.72), channel_id=1, source_target_pairs={{0,8},{4,12},{24,16},{28,20},{1,9},{5,13},{25,17},{29,21},{2,10},{... | collective-permute-start | bytes 983048 | tf_op jit(solution)/shard_map/ppermute | solution.py:470
  58.8 33.6 %collective-permute-start.16 = (bf16[512,384]{1,0:T(8,128)(2,1)S(1)}, bf16[512,384]{1,0:T(8,128)(2,1)S(1)}, u32[]{:S(2)}, u32[]{:S(2)}) collective-permute-start(bf16[512,384]{1,0:T(8,128)(2,1)S(1)} %get-tuple-element.84), channel_id=1, source_target_pairs={{0,8},{4,12},{24,16},{28,20},{1,9},{5,13},{25,17},{29,21},{2,10},{... | collective-permute-start | bytes 1179656 | tf_op jit(solution)/shard_map/ppermute | solution.py:470
  60.1 27.9 %collective-permute-start.4 = (bf16[640,256]{1,0:T(8,128)(2,1)S(1)}, bf16[640,256]{1,0:T(8,128)(2,1)S(1)}, u32[]{:S(2)}, u32[]{:S(2)}) collective-permute-start(bf16[640,256]{1,0:T(8,128)(2,1)S(1)} %get-tuple-element.67), channel_id=1, source_target_pairs={{0,8},{4,12},{24,16},{28,20},{1,9},{5,13},{25,17},{29,21},{2,10},{... | collective-permute-start | bytes 983048 | tf_op jit(solution)/shard_map/ppermute | solution.py:470
  61.4 39.2 %collective-permute-start.13 = (bf16[1152,256]{1,0:T(8,128)(2,1)S(1)}, bf16[1152,256]{1,0:T(8,128)(2,1)S(1)}, u32[]{:S(2)}, u32[]{:S(2)}) collective-permute-start(bf16[1152,256]{1,0:T(8,128)(2,1)S(1)} %get-tuple-element.80), channel_id=1, source_target_pairs={{0,8},{4,12},{24,16},{28,20},{1,9},{5,13},{25,17},{29,21},{2,10},{... | collective-permute-start | bytes 1769480 | tf_op jit(solution)/shard_map/ppermute | solution.py:470
  65.5 27.8 %collective-permute-start.22 = (bf16[512,384]{1,0:T(8,128)(2,1)S(1)}, bf16[512,384]{1,0:T(8,128)(2,1)S(1)}, u32[]{:S(2)}, u32[]{:S(2)}) collective-permute-start(bf16[512,384]{1,0:T(8,128)(2,1)S(1)} %get-tuple-element.89), channel_id=1, source_target_pairs={{8,16},{12,20},{9,17},{13,21},{10,18},{14,22},{11,19},{15,23}} | collective-permute-start | bytes 1179656 | tf_op jit(solution)/shard_map/ppermute | solution.py:470
  72.5 28.8 %collective-permute-start.11 = (bf16[640,256]{1,0:T(8,128)(2,1)S(1)}, bf16[640,256]{1,0:T(8,128)(2,1)S(1)}, u32[]{:S(2)}, u32[]{:S(2)}) collective-permute-start(bf16[640,256]{1,0:T(8,128)(2,1)S(1)} %get-tuple-element.78), channel_id=1, source_target_pairs={{8,16},{12,20},{16,8},{20,12},{9,17},{13,21},{17,9},{21,13},{10,18... | collective-permute-start | bytes 983048 | tf_op jit(solution)/shard_map/ppermute | solution.py:470
  88.0 39.5 %collective-permute-start.24 = (bf16[512,640]{1,0:T(8,128)(2,1)S(1)}, bf16[512,640]{1,0:T(8,128)(2,1)S(1)}, u32[]{:S(2)}, u32[]{:S(2)}) collective-permute-start(bf16[512,640]{1,0:T(8,128)(2,1)S(1)} %collective-permute-done.1.k_ref.k_pair.kc), channel_id=1, source_target_pairs={{0,8},{4,12},{8,16},{12,20},{16,24},{20,28},{1,9},{5,13},{9,17},{1... | collective-permute-start | bytes 1966088 | tf_op jit(solution)/shard_map/ppermute | solution.py:470
  92.4 36.4 %collective-permute-start.21 = (bf16[512,640]{1,0:T(8,128)(2,1)}, bf16[512,640]{1,0:T(8,128)(2,1)S(1)}, u32[]{:S(2)}, u32[]{:S(2)}) collective-permute-start(bf16[512,640]{1,0:T(8,128)(2,1)} %collective-permute-done.2.v_ref.b_ref.v_pair.vc), channel_id=1, source_target_pairs={{16,24},{20,28},{17,25},{21,29},{18,26},{22,30},{19,27},{23,31}} | collective-permute-start | bytes 1966088 | tf_op jit(solution)/shard_map/ppermute | solution.py:470
  93.3 8.8 %collective-permute-start.8 = (bf16[640,256]{1,0:T(8,128)(2,1)S(1)}, bf16[640,256]{1,0:T(8,128)(2,1)S(1)}, u32[]{:S(2)}, u32[]{:S(2)}) collective-permute-start(bf16[640,256]{1,0:T(8,128)(2,1)S(1)} %get-tuple-element.74), channel_id=1, source_target_pairs={{8,16},{12,20},{16,8},{20,12},{9,17},{13,21},{17,9},{21,13},{10,18... | collective-permute-start | bytes 983048 | tf_op jit(solution)/shard_map/ppermute | solution.py:470
  100.6 2.2 %collective-permute-start.5 = (bf16[640,256]{1,0:T(8,128)(2,1)S(1)}, bf16[640,256]{1,0:T(8,128)(2,1)S(1)}, u32[]{:S(2)}, u32[]{:S(2)}) collective-permute-start(bf16[640,256]{1,0:T(8,128)(2,1)S(1)} %get-tuple-element.69), channel_id=1, source_target_pairs={{8,16},{12,20},{16,8},{20,12},{9,17},{13,21},{17,9},{21,13},{10,18... | collective-permute-start | bytes 983048 | tf_op jit(solution)/shard_map/ppermute | solution.py:470
  101.3 28.2 %collective-permute-start.17 = (bf16[512,384]{1,0:T(8,128)(2,1)S(1)}, bf16[512,384]{1,0:T(8,128)(2,1)S(1)}, u32[]{:S(2)}, u32[]{:S(2)}) collective-permute-start(bf16[512,384]{1,0:T(8,128)(2,1)S(1)} %get-tuple-element.86), channel_id=1, source_target_pairs={{8,16},{12,20},{16,8},{20,12},{9,17},{13,21},{17,9},{21,13},{10,18... | collective-permute-start | bytes 1179656 | tf_op jit(solution)/shard_map/ppermute | solution.py:470
  102.1 29.5 %collective-permute-start.14 = (bf16[640,256]{1,0:T(8,128)(2,1)S(1)}, bf16[640,256]{1,0:T(8,128)(2,1)S(1)}, u32[]{:S(2)}, u32[]{:S(2)}) collective-permute-start(bf16[640,256]{1,0:T(8,128)(2,1)S(1)} %get-tuple-element.82), channel_id=1, source_target_pairs={{8,16},{12,20},{16,8},{20,12},{9,17},{13,21},{17,9},{21,13},{10,18... | collective-permute-start | bytes 983048 | tf_op jit(solution)/shard_map/ppermute | solution.py:470
  102.8 70.8 %collective-permute-start.20 = (bf16[2,512,384]{2,1,0:T(8,128)(2,1)S(1)}, bf16[2,512,384]{2,1,0:T(8,128)(2,1)S(1)}, u32[]{:S(2)}, u32[]{:S(2)}) collective-permute-start(bf16[2,512,384]{2,1,0:T(8,128)(2,1)S(1)} %get-tuple-element.88), channel_id=1, source_target_pairs={{0,8},{4,12},{1,9},{5,13},{2,10},{6,14},{3,11},{7,15}} | collective-permute-start | bytes 2359304 | tf_op jit(solution)/shard_map/ppermute | solution.py:470
  127.5 12.5 %collective-permute-start.12 = (bf16[640,256]{1,0:T(8,128)(2,1)S(1)}, bf16[640,256]{1,0:T(8,128)(2,1)S(1)}, u32[]{:S(2)}, u32[]{:S(2)}) collective-permute-start(bf16[640,256]{1,0:T(8,128)(2,1)S(1)} %shard_map.63.made_ref), channel_id=1, source_target_pairs={{8,0},{12,4},{16,24},{20,28},{9,1},{13,5},{17,25},{21,29},{10,2},{... | collective-permute-start | bytes 983048 | tf_op jit(solution)/shard_map/ppermute | solution.py:470
  128.8 4.9 %collective-permute-start.25 = (bf16[512,256]{1,0:T(8,128)(2,1)S(1)}, bf16[512,256]{1,0:T(8,128)(2,1)S(1)}, u32[]{:S(2)}, u32[]{:S(2)}) collective-permute-start(bf16[512,256]{1,0:T(8,128)(2,1)S(1)} %get-tuple-element.94), channel_id=1, source_target_pairs={{8,16},{12,20},{16,8},{20,12},{9,17},{13,21},{17,9},{21,13},{10,18... | collective-permute-start | bytes 786440 | tf_op jit(solution)/shard_map/ppermute | solution.py:470
  129.5 17.5 %collective-permute-start.9 = (bf16[640,256]{1,0:T(8,128)(2,1)S(1)}, bf16[640,256]{1,0:T(8,128)(2,1)S(1)}, u32[]{:S(2)}, u32[]{:S(2)}) collective-permute-start(bf16[640,256]{1,0:T(8,128)(2,1)S(1)} %shard_map.60.made_ref), channel_id=1, source_target_pairs={{8,0},{12,4},{16,24},{20,28},{9,1},{13,5},{17,25},{21,29},{10,2},{... | collective-permute-start | bytes 983048 | tf_op jit(solution)/shard_map/ppermute | solution.py:470
  131.6 22.4 %collective-permute-start.6 = (bf16[640,256]{1,0:T(8,128)(2,1)S(1)}, bf16[640,256]{1,0:T(8,128)(2,1)S(1)}, u32[]{:S(2)}, u32[]{:S(2)}) collective-permute-start(bf16[640,256]{1,0:T(8,128)(2,1)S(1)} %shard_map.57.made_ref), channel_id=1, source_target_pairs={{8,0},{12,4},{16,24},{20,28},{9,1},{13,5},{17,25},{21,29},{10,2},{... | collective-permute-start | bytes 983048 | tf_op jit(solution)/shard_map/ppermute | solution.py:470
  133.7 25.9 %collective-permute-start.15 = (bf16[640,256]{1,0:T(8,128)(2,1)S(1)}, bf16[640,256]{1,0:T(8,128)(2,1)S(1)}, u32[]{:S(2)}, u32[]{:S(2)}) collective-permute-start(bf16[640,256]{1,0:T(8,128)(2,1)S(1)} %shard_map.66.made_ref), channel_id=1, source_target_pairs={{8,0},{12,4},{16,24},{20,28},{9,1},{13,5},{17,25},{21,29},{10,2},{... | collective-permute-start | bytes 983048 | tf_op jit(solution)/shard_map/ppermute | solution.py:470
  140.0 42.2 %collective-permute-start.27 = (bf16[2,512,256]{2,1,0:T(8,128)(2,1)S(1)}, bf16[2,512,256]{2,1,0:T(8,128)(2,1)S(1)}, u32[]{:S(2)}, u32[]{:S(2)}) collective-permute-start(bf16[2,512,256]{2,1,0:T(8,128)(2,1)S(1)} %get-tuple-element.95), channel_id=1, source_target_pairs={{0,8},{4,12},{1,9},{5,13},{2,10},{6,14},{3,11},{7,15}} | collective-permute-start | bytes 1572872 | tf_op jit(solution)/shard_map/ppermute | solution.py:470
  147.0 26.6 %collective-permute-start.18 = (bf16[512,384]{1,0:T(8,128)(2,1)S(1)}, bf16[512,384]{1,0:T(8,128)(2,1)S(1)}, u32[]{:S(2)}, u32[]{:S(2)}) collective-permute-start(bf16[512,384]{1,0:T(8,128)(2,1)S(1)} %shard_map.69.refs_4_), channel_id=1, source_target_pairs={{8,0},{12,4},{16,24},{20,28},{9,1},{13,5},{17,25},{21,29},{10,2},{... | collective-permute-start | bytes 1179656 | tf_op jit(solution)/shard_map/ppermute | solution.py:470
  154.0 28.2 %collective-permute-start.28 = (bf16[512,256]{1,0:T(8,128)(2,1)S(1)}, bf16[512,256]{1,0:T(8,128)(2,1)S(1)}, u32[]{:S(2)}, u32[]{:S(2)}) collective-permute-start(bf16[512,256]{1,0:T(8,128)(2,1)S(1)} %get-tuple-element.96), channel_id=1, source_target_pairs={{8,16},{12,20},{9,17},{13,21},{10,18},{14,22},{11,19},{15,23}} | collective-permute-start | bytes 786440 | tf_op jit(solution)/shard_map/ppermute | solution.py:470
  159.6 22.6 %collective-permute-start.26 = (bf16[512,256]{1,0:T(8,128)(2,1)S(1)}, bf16[512,256]{1,0:T(8,128)(2,1)S(1)}, u32[]{:S(2)}, u32[]{:S(2)}) collective-permute-start(bf16[512,256]{1,0:T(8,128)(2,1)S(1)} %shard_map.74.refs_4_), channel_id=1, source_target_pairs={{8,0},{12,4},{16,24},{20,28},{9,1},{13,5},{17,25},{21,29},{10,2},{... | collective-permute-start | bytes 786440 | tf_op jit(solution)/shard_map/ppermute | solution.py:470
  176.1 23.2 %collective-permute-start.29 = (bf16[512,384]{1,0:T(8,128)(2,1)S(1)}, bf16[512,384]{1,0:T(8,128)(2,1)S(1)}, u32[]{:S(2)}, u32[]{:S(2)}) collective-permute-start(bf16[512,384]{1,0:T(8,128)(2,1)S(1)} %shard_map.78), channel_id=1, source_target_pairs={{0,4},{4,0},{8,12},{12,8},{16,20},{20,16},{24,28},{28,24},{1,5},{5... | collective-permute-start | bytes 1179656 | tf_op jit(solution)/shard_map/ppermute | solution.py:470
  184.3 15.0 %collective-permute-start.30 = (bf16[512,256]{1,0:T(8,128)(2,1)S(1)}, bf16[512,256]{1,0:T(8,128)(2,1)S(1)}, u32[]{:S(2)}, u32[]{:S(2)}) collective-permute-start(bf16[512,256]{1,0:T(8,128)(2,1)S(1)} %shard_map.80), channel_id=1, source_target_pairs={{0,4},{4,0},{8,12},{12,8},{16,20},{20,16},{24,28},{28,24},{1,5},{5... | collective-permute-start | bytes 786440 | tf_op jit(solution)/shard_map/ppermute | solution.py:470
  (5 other events, 42.0 us)
